TPU v7x, 32 devices: a whole 2x2x4 slice. The times are simulated.
32 devices in a mesh: group: 2 (over x), dev: 8 (over z, y), head: 2 (over core).
Axes of the slice: x: 2, y: 2, z: 4, core: 2. Of those that a mesh axis runs over, the one named last changes fastest.
Arguments:
- residual_in: bfloat16 [2048, 4096], P(('group', 'dev')), parts along dimension 0, may hold values from -6 to 6
- queries: bfloat16 [2048, 48, 128], P(('group', 'dev'), 'head'), parts along dimension 0, may hold values from -400 to 400
- key_cache: bfloat16 [32, 2048, 4, 128], P(('group', 'dev'), None, 'head'), parts along dimension 0, may hold values from -6 to 6
- value_cache: bfloat16 [32, 2048, 4, 128], P(('group', 'dev'), None, 'head'), parts along dimension 0, may hold values from -6 to 6
- new_keys: bfloat16 [2048, 4, 128], P(('group', 'dev'), 'head'), parts along dimension 0, may hold values from -6 to 6
- new_values: bfloat16 [2048, 4, 128], P(('group', 'dev'), 'head'), parts along dimension 0, may hold values from -6 to 6
- prefix_len: int32 [32], P(('group', 'dev')), parts along dimension 0, may hold values from 512 to 2048
- o_weight: bfloat16 [6144, 4096], P('head', 'dev'), may hold values from -0.078125 to 0.078125
- norm_gain: float32 [4096], replicated, may hold values from 0.5 to 1.5
- expert_ids: int32 [2048, 8], P(('group', 'dev')), parts along dimension 0, may hold values from 0 to 15, all different within a row; in each aligned block of 128 rows (0 to 127, 128 to 255, ...) at most 80 rows name the same one
- route_weights: float32 [2048, 8], P(('group', 'dev')), parts along dimension 0, may hold values from 0.1 to 0.4
- capacity: int32 [32], P('group'), parts along dimension 0, may hold values from 256 to 640
- gate_w: bfloat16 [16, 4096, 1408], P('dev', None, 'head'), may hold values from -0.09375 to 0.09375
- up_w: bfloat16 [16, 4096, 1408], P('dev', None, 'head'), may hold values from -0.09375 to 0.09375
- down_w: bfloat16 [16, 1408, 4096], P('dev', 'head'), may hold values from -0.15625 to 0.15625
Outputs:
- hidden: bfloat16 [2048, 4096], P(('group', 'dev'), 'head'), parts along dimension 0
- moe_out: bfloat16 [2048, 4096], P(('group', 'dev'), 'head'), parts along dimension 0
There are 2 independent parts, one for each index of `group`. A program takes and returns all parts, laid end to end along the dimension named above; an argument that names none is the same for every part. Nothing has to cross between parts.
Inputs may be any that keep to these rules, and one draw needn't show every extreme that they name: `expert_ids`: each row names 8 different experts; among the tokens of one index of dev no expert is named more than 80 times.
All inputs are finite; a program needn't handle non-finite values.
Results may differ from a plain program's by a relative error of at most 0.014.
Values may be sent and summed in bfloat16 or wider, within the bound.
No kernel may reach another device: no remote copies, remote signals or barrier semaphores. Data moves between devices by JAX's collectives and lax.ppermute only.
A program may use at most 128 MiB of HBM per device.

v0:
```python
import functools

import jax
import jax.numpy as jnp
from jax import lax
from jax.experimental import pallas as pl
from jax.experimental.pallas import tpu as pltpu
from jax.sharding import PartitionSpec as P


VMEM = 58 << 20
LAST = (((1,), (1,)), ((), ()))


def cost(flops, moved, trans=0):
    return pl.CostEstimate(flops=int(flops), bytes_accessed=int(moved), transcendentals=int(trans))


def attend_body(len_ref, q_ref, k_ref, v_ref, nk_ref, nv_ref, o_ref, ks, vs, *, seq, kv, heads, hd, step, kb):
    tok = q_ref.shape[0]
    count = k_ref.shape[0] // kv
    length = len_ref[seq]
    c = hd ** (-0.5) * 1.4426950408889634
    n = kb * kv
    r = lax.broadcasted_iota(jnp.int32, (n, n), 0); cc = lax.broadcasted_iota(jnp.int32, (n, n), 1)
    perm = (cc == (r % kb) * kv + r // kb).astype(jnp.bfloat16)
    for b in range(count // kb):
        for src, dst in ((k_ref, ks), (v_ref, vs)):
            t = jnp.dot(perm, src[b * n:(b + 1) * n], preferred_element_type=jnp.float32).astype(jnp.bfloat16)
            for h in range(kv):
                dst[h, b * kb:(b + 1) * kb] = t[h * kb:(h + 1) * kb]
    valid = lax.broadcasted_iota(jnp.int32, (1, count), 1) < length
    wide = step * hd
    row = lax.broadcasted_iota(jnp.int32, (step * tok, tok), 0) % tok
    seen = lax.broadcasted_iota(jnp.int32, (step * tok, tok), 1) <= row

    def one(i, _):
        h = i * step // heads
        at = pl.ds(pl.multiple_of(i * wide, wide), wide)
        mine = pl.ds(pl.multiple_of(h * hd, hd), hd)
        q = q_ref[:, at]
        q = jnp.concatenate([q[:, j * hd : (j + 1) * hd] for j in range(step)], 0)
        s = lax.dot_general(q, ks[h], LAST, preferred_element_type=jnp.float32)
        f = lax.dot_general(q, nk_ref[:, mine], LAST, preferred_element_type=jnp.float32)
        s = jnp.where(valid, s, -1e30)
        f = jnp.where(seen, f, -1e30)
        m = jnp.maximum(jnp.max(s, 1, keepdims=True), jnp.max(f, 1, keepdims=True))
        p = jnp.exp2((s - m) * c)
        pf = jnp.exp2((f - m) * c)
        total = jnp.sum(p, 1, keepdims=True) + jnp.sum(pf, 1, keepdims=True)
        o = jnp.dot(p.astype(jnp.bfloat16), vs[h], preferred_element_type=jnp.float32)
        o = o + jnp.dot(pf.astype(jnp.bfloat16), nv_ref[:, mine], preferred_element_type=jnp.float32)
        o = (o / total).astype(jnp.bfloat16)
        o_ref[:, at] = jnp.concatenate([o[j * tok : (j + 1) * tok] for j in range(step)], 1)
        return 0

    lax.fori_loop(0, kv * heads // step, one, 0)


def attend(q, keys, values, fk, fv, lengths, seq, kv, hd, step=4):
    tok, wide = q.shape
    rows = keys.shape[1]
    heads = wide // hd // kv
    whole = lambda a: pl.BlockSpec(a.shape, lambda i, l: (0,) * a.ndim)
    kspec = pl.BlockSpec((None, rows, hd), lambda i, l: (seq, 0, 0))
    return pl.pallas_call(
        functools.partial(attend_body, seq=seq, kv=kv, heads=heads, hd=hd, step=step, kb=128),
        out_shape=jax.ShapeDtypeStruct((tok, wide), jnp.bfloat16),
        grid_spec=pltpu.PrefetchScalarGridSpec(num_scalar_prefetch=1, grid=(1,),
            in_specs=[whole(q), kspec, kspec, whole(fk), whole(fv)], out_specs=whole(q),
            scratch_shapes=[pltpu.VMEM((kv, rows // kv, hd), jnp.bfloat16)] * 2),
        compiler_params=pltpu.CompilerParams(vmem_limit_bytes=VMEM),
        cost_estimate=cost(4 * tok * wide * (rows // kv), 4 * rows * hd, tok * wide // hd * (rows // kv)), name="attend")(lengths, q, keys, values, fk, fv)


def project_body(order_ref, w_ref, *refs, nz):
    slots, refs = refs[:nz], refs[nz:]
    pieces, (keep_ref, send_ref, x) = refs[:-3], refs[-3:]
    head, y, g = order_ref[nz], order_ref[nz + 1], order_ref[nz + 2]
    rows, depth = slots[0].shape
    half = rows // 2
    cw = w_ref.shape[1]
    for j in range(nz):
        x[j * rows : (j + 1) * rows] = slots[j][...]

    def put(out, at):
        for j in range(nz):
            low = out[j * rows : j * rows + half]
            high = out[j * rows + half : (j + 1) * rows]
            keep_ref[order_ref[j], :, at] = jnp.where(head == 0, low, high)
            send_ref[order_ref[j], :, at] = jnp.where(head == 0, high, low).astype(jnp.bfloat16)

    at = lambda i: pl.ds(pl.multiple_of(i * cw, cw), cw)
    put(jnp.dot(x[...], w_ref[...], preferred_element_type=jnp.float32), at(y))
    if pieces:
        middle, near, far = pieces
        end = near.shape[0]
        edge = lambda i: pl.ds(pl.multiple_of(i * (depth - end), 128), end)
        out = jnp.dot(x[:, end : depth - end], middle[...], preferred_element_type=jnp.float32)
        out = out + jnp.dot(x[:, edge(g)], near[...], preferred_element_type=jnp.float32)
        out = out + jnp.dot(x[:, edge(1 - g)], far[...], preferred_element_type=jnp.float32)
        put(out, at(1 - y))


def project(slots, w, pieces, order):
    nz = len(slots)
    rows, depth = slots[0].shape
    cols = w.shape[1] * (2 if pieces else 1)
    whole = lambda a: pl.BlockSpec(a.shape, lambda i, o: (0,) * a.ndim)
    shape = (nz, rows // 2, cols)
    return pl.pallas_call(
        functools.partial(project_body, nz=nz),
        out_shape=(jax.ShapeDtypeStruct(shape, jnp.float32), jax.ShapeDtypeStruct(shape, jnp.bfloat16)),
        grid_spec=pltpu.PrefetchScalarGridSpec(
            num_scalar_prefetch=1,
            grid=(1,),
            in_specs=[whole(a) for a in (w, *slots, *pieces)],
            out_specs=[pl.BlockSpec(shape, lambda i, o: (0, 0, 0))] * 2,
            scratch_shapes=[pltpu.VMEM((nz * rows, depth), jnp.bfloat16)],
        ),
        compiler_params=pltpu.CompilerParams(vmem_limit_bytes=VMEM),
        cost_estimate=cost(2 * nz * rows * depth * cols, 2 * (nz * rows * depth + depth * cols)),
        name="project",
    )(order, w, *slots, *pieces)


def expert_body(order_ref, wt_ref, gain_ref, gate_hbm, up_hbm, down_hbm, *refs, nz, eps, show):
    p, refs = refs[:4], refs[4:]
    theirs_ref, ours_ref, refs = refs[0], refs[1], refs[2:]
    if show:
        hid_ref, refs = refs[0], refs[1:]
    wbuf, dbuf, xs, res, act_t, acts, r_t, ss, first_sem, block_sem, down_sem = refs
    head, me = order_ref[nz], order_ref[nz + 3]
    _, part, cw = p[0].shape
    rows = 2 * nz * part
    half = nz // 2
    experts, ff, _ = gate_hbm.shape
    cols = dbuf.shape[3]
    span = lambda c: pl.ds(pl.multiple_of(c * cw, cw), cw)
    sources = (gate_hbm, up_hbm)

    def first(j):
        at = span(order_ref[j])
        return [
            pltpu.make_async_copy(src.at[0, :, at], wbuf.at[0, i, :, at], first_sem.at[i, j])
            for i, src in enumerate(sources)
        ]

    def block(e):
        return [
            pltpu.make_async_copy(src.at[e], wbuf.at[e % 2, i], block_sem.at[i, e % 2])
            for i, src in enumerate(sources)
        ]

    def down_half(i):
        h = 1 - head if i == 0 else head
        at = pl.ds(pl.multiple_of(h * cols, cols), cols)
        return pltpu.make_async_copy(down_hbm.at[:, :, at], dbuf.at[i], down_sem.at[i])

    def start(copies):
        for c in copies:
            c.start()

    def wait(copies):
        for c in copies:
            c.wait()

    for j in range(nz):
        start(first(j))
    if experts > 1:
        start(block(1))
    down_half(0).start()

    def chunk(j, own, other, begin):
        c = order_ref[j]
        at = span(c)
        v = jnp.concatenate([own[...], other[...]], 0).reshape(rows, cw).astype(jnp.float32)
        xs[:, at] = (v * gain_ref[:, at]).astype(jnp.bfloat16)
        wait(first(j))

        def product(i, _):
            out = lax.dot_general(wbuf[0, i, :, at], xs[:, at], LAST, preferred_element_type=jnp.float32)
            res[i] = out if begin else res[i] + out
            return 0

        lax.fori_loop(0, 2, product, 0)
        v = v * v
        total = v[:, :128]
        for i in range(128, cw, 128):
            total = total + v[:, i : i + 128]
        ss[...] = total if begin else ss[...] + total
        if show:

            @pl.when(c // half == head)
            def _():
                to = span(c % half)
                hid_ref[0, :, to] = own[me]
                hid_ref[1, :, to] = other[me]

    chunk(0, p[0], p[2], True)

    def later(j, _):
        chunk(j, p[1].at[j - 1], p[3].at[j - 1], False)
        return 0

    lax.fori_loop(1, nz, later, 0)
    r_t[...] = lax.rsqrt(jnp.sum(ss[...].T, axis=0, keepdims=True) / (nz * cw) + eps)

    def activate(e):
        w = wt_ref[e : e + 1, :] * r_t[...]
        g = res[0] * r_t[...]
        act_t[e * ff : (e + 1) * ff, :] = (g / (1 + jnp.exp(-g)) * (res[1] * w)).astype(jnp.bfloat16)

    activate(0)
    down_half(1).start()
    for e in range(1, experts):
        wait(block(e))

        def product(i, _, e=e):
            res[i] = lax.dot_general(wbuf[e % 2, i], xs[...], LAST, preferred_element_type=jnp.float32)
            return 0

        lax.fori_loop(0, 2, product, 0)
        if e + 1 < experts:
            start(block(e + 1))
        activate(e)
    acts[...] = act_t[...].T
    step = min(1024, cols)
    for i, out in ((0, theirs_ref), (1, ours_ref)):
        down_half(i).wait()

        def columns(n, _, i=i, out=out):
            at = pl.ds(pl.multiple_of(n * step, step), step)
            acc = jnp.dot(acts[...], dbuf[i, :, :, at].reshape(-1, step), preferred_element_type=jnp.float32)
            for k in range(2):
                out[:, k, :, at] = acc[k * nz * part : (k + 1) * nz * part].reshape(nz, part, step).astype(out.dtype)
            return 0

        lax.fori_loop(0, cols // step, columns, 0)


def expert(p, wt, gain, gate_t, up_t, down_w, order, show):
    nz, part, cw = p[0].shape
    experts, ff, depth = gate_t.shape
    rows = 2 * nz * part
    cols = down_w.shape[2] // 2
    out = jax.ShapeDtypeStruct((nz, 2, part, cols), jnp.bfloat16)
    shapes = [out, out]
    if show:
        shapes.append(jax.ShapeDtypeStruct((2, part, nz // 2 * cw), jnp.bfloat16))
    vmem, hbm = pl.BlockSpec(memory_space=pltpu.VMEM), pl.BlockSpec(memory_space=pl.ANY)
    return pl.pallas_call(
        functools.partial(expert_body, nz=nz, eps=1e-5, show=show),
        out_shape=shapes,
        in_specs=[pl.BlockSpec(memory_space=pltpu.SMEM), vmem, vmem, hbm, hbm, hbm] + [vmem] * 4,
        out_specs=[vmem] * len(shapes),
        scratch_shapes=[
            pltpu.VMEM((min(2, experts), 2, ff, depth), jnp.bfloat16),
            pltpu.VMEM((2, experts, ff, cols), jnp.bfloat16),
            pltpu.VMEM((rows, depth), jnp.bfloat16),
            pltpu.VMEM((2, ff, rows), jnp.float32),
            pltpu.VMEM((experts * ff, rows), jnp.bfloat16),
            pltpu.VMEM((rows, experts * ff), jnp.bfloat16),
            pltpu.VMEM((1, rows), jnp.float32),
            pltpu.VMEM((rows, 128), jnp.float32),
            pltpu.SemaphoreType.DMA((2, nz)),
            pltpu.SemaphoreType.DMA((2, 2)),
            pltpu.SemaphoreType.DMA((2,)),
        ],
        compiler_params=pltpu.CompilerParams(vmem_limit_bytes=VMEM),
        cost_estimate=cost(6 * rows * depth * ff * experts, 6 * depth * ff * experts),
        name="expert",
    )(order, wt, gain, gate_t, up_t, down_w, *p)


def settle_body(order_ref, ours_ref, theirs_ref, *refs, nz, adds, spread):
    extra, outs = refs[:adds], refs[adds:]

    def total(zz, i):
        out = ours_ref[zz, i].astype(jnp.float32) + theirs_ref[zz, 1 - i].astype(jnp.float32)
        for ref in extra:
            out = out + ref[zz, i].astype(jnp.float32)
        return out.astype(jnp.bfloat16)

    for j in range(nz):
        zz = lax.rem(order_ref[nz + 3] + j, nz) if spread else j
        for i in range(2):
            if spread:
                outs[j][i] = total(zz, i)
            else:
                outs[0][j, i] = total(zz, i)


def settle(ours, theirs, order, extra, spread, steps=2):
    nz, two, part, cols = ours.shape
    nb = cols // steps
    block = pl.BlockSpec((nz, two, part, nb), lambda i, o: (0, 0, 0, i))
    if spread:
        shapes = [jax.ShapeDtypeStruct((two, part, cols), jnp.bfloat16)] * nz
        specs = [pl.BlockSpec((two, part, nb), lambda i, o: (0, 0, i))] * nz
    else:
        shapes, specs = [jax.ShapeDtypeStruct(ours.shape, jnp.bfloat16)], [block]
    return pl.pallas_call(
        functools.partial(settle_body, nz=nz, adds=len(extra), spread=spread),
        out_shape=shapes,
        grid_spec=pltpu.PrefetchScalarGridSpec(
            num_scalar_prefetch=1, grid=(steps,), in_specs=[block] * (2 + len(extra)), out_specs=specs
        ),
        compiler_params=pltpu.CompilerParams(vmem_limit_bytes=VMEM),
        cost_estimate=cost(4 * ours.size, 2 * ours.size * (3 + len(extra))),
        name="settle",
    )(order, ours, theirs, *extra)


def on_device(
    residual_in, queries, key_cache, value_cache, new_keys, new_values, prefix_len, o_weight,
    norm_gain, expert_ids, route_weights, capacity, gate_w, up_w, down_w, *, nz, ny,
):
    n = nz * ny
    d, head, g = lax.axis_index("dev"), lax.axis_index("head"), lax.axis_index("group")
    z, y = d // ny, d % ny
    tok, q_heads, hd = queries.shape
    seqs = key_cache.shape[0]
    resp = tok // seqs
    part = resp // 2
    f32, bf16 = jnp.float32, jnp.bfloat16

    def shift(x, k):
        pairs = [(a * ny + b, (a + k) % nz * ny + b) for a in range(nz) for b in range(ny)]
        return lax.ppermute(x, "dev", pairs)

    def across(x):
        return lax.ppermute(x, "dev", [(a * ny + b, a * ny + (b + 1) % ny) for a in range(nz) for b in range(ny)])

    partner = lambda x: lax.ppermute(x, "head", [(0, 1), (1, 0)])
    groups = lax.axis_size("group")
    twin = lambda x: lax.ppermute(x, "group", [(i, i ^ 1) for i in range(groups)])

    slot_z = jnp.stack([(z - j) % nz for j in range(nz)])
    order = jnp.concatenate([slot_z, jnp.stack([head, y, g % 2, z])]).astype(jnp.int32)

    w_pieces = ()
    if ny > 1:
        depth = o_weight.shape[0]
        end = depth // 640 * 128
        near = across(lax.dynamic_slice_in_dim(o_weight, g % 2 * (depth - end), end, 0))
        middle = across(o_weight[end : depth - end])
        far = twin(near)
        w_pieces = (middle, near, far)

    width = residual_in.shape[1]
    cw = width // nz
    res = lax.dynamic_index_in_dim(residual_in.reshape(seqs, 2, part, width), head, 1, False)
    columns = lambda zz: lax.dynamic_slice_in_dim(res, zz % nz * cw, cw, 2)

    def line(x):
        forward, back = nz // 2, nz - 1 - nz // 2
        up, down_ = [x], [x]
        for i in range(max(forward, back)):
            if i < forward:
                up.append(shift(up[-1], 1))
            if i < back:
                down_.append(shift(down_[-1], -1))
        return up + down_[:0:-1]

    res_slots = jnp.stack([columns(z)] + [shift(columns(z + k), k) for k in range(1, nz)])
    res_line = jnp.stack([lax.dynamic_index_in_dim(res_slots, (z - a) % nz, 0, False) for a in range(nz)])

    q_flat = queries.reshape(seqs, resp, q_heads * hd)
    flat = lambda x: x.reshape(x.shape[0], -1)
    kv = key_cache.shape[2]
    keys, values = (c.reshape(seqs, -1, hd) for c in (key_cache, value_cache))
    lines = []
    for s in range(seqs):
        rows = slice(s * resp, (s + 1) * resp)
        att = attend(q_flat[s], keys, values, flat(new_keys[rows]), flat(new_values[rows]), prefix_len, s, kv, hd)
        lines.append(line(att))

    packed = jnp.concatenate([expert_ids.astype(f32), route_weights], 1)
    pair = packed[None] if ny == 1 else jnp.stack([packed, across(packed)])
    got = jnp.concatenate([pair] + [shift(pair, k) for k in range(1, nz)], 0)

    slot_dev = jnp.stack([(z - j) % nz * ny + (y + i) % ny for j in range(nz) for i in range(ny)])
    table = jnp.zeros((n, tok, packed.shape[1]), f32).at[slot_dev].set(got).reshape(n * tok, -1)
    top = expert_ids.shape[1]
    ids, weights = table[:, :top].astype(jnp.int32), table[:, top:]
    local = gate_w.shape[0]
    mine = d * local + jnp.arange(local)
    hits = ids[:, :, None] == mine[None, None, :]
    named = jnp.any(hits, 1)
    earlier = jnp.cumsum(named.astype(jnp.int32), 0) - named
    limit = lax.dynamic_slice_in_dim(capacity, d * local, local)
    wt = jnp.where(earlier < limit[None], jnp.sum(jnp.where(hits, weights[:, :, None], 0.0), 1), 0.0)
    wt = wt.reshape(nz, ny, seqs, 2, part, local).transpose(1, 2, 5, 3, 0, 4)
    wt = jnp.where(head == 0, wt, wt[:, :, :, ::-1]).reshape(ny, seqs, local, 2 * nz * part)
    wt = [lax.dynamic_index_in_dim(wt, (y + i) % ny, 0, False) for i in range(ny)]

    gain = norm_gain[None]
    gate_t, up_t = gate_w.swapaxes(1, 2), up_w.swapaxes(1, 2)
    tie = lambda a, b: lax.optimization_barrier((a, b))[0]

    planes = []
    for s in range(seqs):
        keep, send = project(lines[s], o_weight, w_pieces, order)
        if planes:
            keep = tie(keep, planes[-1][0][0])
        projected = (keep + partner(send).astype(f32)).astype(bf16)
        hidden = (res_line[:, s].astype(f32) + projected.astype(f32)).astype(bf16)
        later = jnp.stack([shift(hidden, k) for k in range(1, nz)])
        rows_of = [(hidden, later)]
        if ny > 1:
            head_part = across(hidden)
            rows_of.append((head_part, across(later)))
        pieces = []
        for a, b in rows_of:
            pa = partner(a)
            pieces.append((a, b, pa, partner(b)))
        planes.append(pieces)

    hidden_parts, moe_parts = [None] * seqs, [None] * seqs
    summed = {}

    def run(s, i):
        out = expert(planes[s][i], wt[i][s], gain, gate_t, up_t, down_w, order, show=i == 0)
        if i == 0:
            hidden_parts[s] = out[2]
        summed[s, i] = (out[1], partner(out[0]))

    def other_plane(s):
        ours, theirs = summed[s, 1]
        summed[s, 1] = across((ours.astype(f32) + theirs[:, ::-1].astype(f32)).astype(bf16))

    def finish(s):
        extra = (summed[s, 1],) if ny > 1 else ()
        terms = settle(*summed[s, 0], order, extra, True)
        moved = {}
        for step, count in ((1, nz // 2), (-1, nz - 1 - nz // 2)):
            for i, k in enumerate(range(count, 0, -1)):
                term = terms[step * k]
                if i:
                    term = (term.astype(f32) + moved[step].astype(f32)).astype(bf16)
                moved[step] = shift(term, step)
        final = terms[0].astype(f32)
        for got in moved.values():
            final = final + got.astype(f32)
        moe_parts[s] = final.astype(bf16)

    if ny == 1:
        for s in range(seqs):
            run(s, 0)
            finish(s)
    else:
        for s in range(seqs):
            first_plane = 1 if s and s == seqs - 1 else 0
            run(s, first_plane)
            if first_plane:
                other_plane(s)
            run(s, 1 - first_plane)
            if not first_plane:
                other_plane(s)
            finish(s)
    place = lambda parts: jnp.stack([jnp.where(head == 0, p, p[::-1]) for p in parts]).reshape(tok, -1)
    return place(hidden_parts), place(moe_parts)


def solution(mesh):
    in_specs = (
        P(("group", "dev"), None),
        P(("group", "dev"), "head", None),
        P(("group", "dev"), None, "head", None),
        P(("group", "dev"), None, "head", None),
        P(("group", "dev"), "head", None),
        P(("group", "dev"), "head", None),
        P(("group", "dev")),
        P("head", "dev"),
        P(),
        P(("group", "dev"), None),
        P(("group", "dev"), None),
        P("group"),
        P("dev", None, "head"),
        P("dev", None, "head"),
        P("dev", "head", None),
    )
    out_specs = (P(("group", "dev"), "head"), P(("group", "dev"), "head"))
    n = mesh.shape["dev"]
    spots = [getattr(c, "coords", (0, 0, i)) for i, c in enumerate(mesh.devices[0, :, 0])]
    ny = n // len({p[2] for p in spots})

    def body(*args):
        return on_device(*args, nz=n // ny, ny=ny)

    return jax.shard_map(body, mesh=mesh, in_specs=in_specs, out_specs=out_specs, check_vma=False)
```

profile of v0, /device:TPU:0, one launch (start us, length us, event | category | flops | bytes accessed | tf_op | source)
XLA Modules:
  0.0 337.7 jit_solution(12149554843118700385)
XLA Ops:
  9.6 12.1 %attend.2.refs_0_ = bf16[64,3072]{1,0:T(8,128)(2,1)} custom-call(s32[2]{0:T(128)} %len_ref.3, bf16[64,3072]{1,0:T(8,128)(2,1)} %bitcast.141, bf16[2,4096,128]{2,1,0:T(8,128)(2,1)} %bitcast.160, bf16[2,4096,128]{2,1,0:T(8,128)(2,1)} %bitcast.162, bf16[64,256]{1,0:T(8,128)(2,1)} %get-tuple-element.73.nk_ref, bf16[64,256]{1,0:T(8,128)(2,1)} %get-tuple-element.72.nv_ref), custom_call_target="tpu_custom_call" | custom-call | flops 1610612736 | bytes 2097152 | tf_op jit(solution)/shard_map/attend/pallas_call | solution.py:66
  33.8 12.1 %attend.3.refs_0_ = bf16[64,3072]{1,0:T(8,128)(2,1)} custom-call(s32[2]{0:T(128)} %len_ref.3, bf16[64,3072]{1,0:T(8,128)(2,1)} %bitcast.140, bf16[2,4096,128]{2,1,0:T(8,128)(2,1)} %bitcast.161, bf16[2,4096,128]{2,1,0:T(8,128)(2,1)} %bitcast.163, bf16[64,256]{1,0:T(8,128)(2,1)} %get-tuple-element.71.nk_ref, bf16[64,256]{1,0:T(8,128)(2,1)} %get-tuple-element.70.nv_ref), custom_call_target="tpu_custom_call" | custom-call | flops 1610612736 | bytes 2097152 | tf_op jit(solution)/shard_map/attend/pallas_call | solution.py:66
  46.6 17.5 %collective-permute-done = f32[128,16]{0,1:T(8,128)} collective-permute-done((f32[128,16]{0,1:T(8,128)}, f32[128,16]{0,1:T(8,128)}, u32[]{:S(2)}, u32[]{:S(2)}) %collective-permute-start) | collective-permute-done | bytes 8224 | tf_op jit(solution)/shard_map/ppermute | solution.py:333
  77.2 13.7 %collective-permute-done.3 = f32[2,128,16]{1,2,0:T(8,128)S(1)} collective-permute-done((f32[2,128,16]{1,2,0:T(8,128)S(1)}, f32[2,128,16]{1,2,0:T(8,128)S(1)}, u32[]{:S(2)}, u32[]{:S(2)}) %collective-permute-start.3) | collective-permute-done | bytes 16416 | tf_op jit(solution)/shard_map/ppermute | solution.py:330
  91.6 3.9 %collective-permute-start.21 = (bf16[64,3072]{1,0:T(8,128)(2,1)}, bf16[64,3072]{1,0:T(8,128)(2,1)S(1)}, u32[]{:S(2)}, u32[]{:S(2)}) collective-permute-start(bf16[64,3072]{1,0:T(8,128)(2,1)} %attend.3.refs_0_), channel_id=1, source_target_pairs={{0,12},{2,14},{4,0},{6,2},{8,4},{10,6},{12,8},{14,10},{1,13},{3,15... | collective-permute-start | bytes 1179656 | tf_op jit(solution)/shard_map/ppermute | solution.py:330
  99.4 6.6 %project.2 = (f32[4,32,1024]{2,1,0:T(8,128)}, bf16[4,32,1024]{2,1,0:T(8,128)(2,1)}) custom-call(s32[8]{0:T(128)} %concatenate.29.order_ref, bf16[3072,512]{1,0:T(8,128)(2,1)} %w_ref.3, bf16[64,3072]{1,0:T(8,128)(2,1)} %attend.2.refs_0_, bf16[64,3072]{1,0:T(8,128)(2,1)} %collective-permute-done.7.refs_1_, bf16[64,3072]{1,0:T(8,128)(2,1)} %collective-permute-done.8.refs_2_, ...), custom_call_target="tpu_custom_call" | custom-call | flops 1610612736 | bytes 7864320 | tf_op jit(solution)/shard_map/project/pallas_call | solution.py:111
  118.5 4.9 %collective-permute-done.14 = bf16[4,32,1024]{2,1,0:T(8,128)(2,1)S(1)} collective-permute-done((bf16[4,32,1024]{2,1,0:T(8,128)(2,1)S(1)}, bf16[4,32,1024]{2,1,0:T(8,128)(2,1)S(1)}, u32[]{:S(2)}, u32[]{:S(2)}) %collective-permute-start.14) | collective-permute-done | bytes 262176 | tf_op jit(solution)/shard_map/ppermute | solution.py:330
  123.4 11.2 %collective-permute-done.15 = bf16[4,32,1024]{2,1,0:T(8,128)(2,1)S(1)} collective-permute-done((bf16[4,32,1024]{2,1,0:T(8,128)(2,1)S(1)}, bf16[4,32,1024]{2,1,0:T(8,128)(2,1)S(1)}, u32[]{:S(2)}, u32[]{:S(2)}) %collective-permute-start.15) | collective-permute-done | bytes 262176 | tf_op jit(solution)/shard_map/ppermute | solution.py:330
  137.4 4.9 %collective-permute-done.20.refs_2_ = bf16[64,3072]{1,0:T(8,128)(2,1)S(1)} collective-permute-done((bf16[64,3072]{1,0:T(8,128)(2,1)}, bf16[64,3072]{1,0:T(8,128)(2,1)S(1)}, u32[]{:S(2)}, u32[]{:S(2)}) %collective-permute-start.20) | collective-permute-done | bytes 393248 | tf_op jit(solution)/shard_map/ppermute | solution.py:330
  143.0 6.6 %project.3 = (f32[4,32,1024]{2,1,0:T(8,128)}, bf16[4,32,1024]{2,1,0:T(8,128)(2,1)}) custom-call(s32[8]{0:T(128)} %concatenate.29.order_ref, bf16[3072,512]{1,0:T(8,128)(2,1)} %w_ref.3, bf16[64,3072]{1,0:T(8,128)(2,1)} %attend.3.refs_0_, bf16[64,3072]{1,0:T(8,128)(2,1)} %collective-permute-done.19.refs_1_, bf16[64,3072]{1,0:T(8,128)(2,1)} %copy-done.19, ...), custom_call_target="tpu_custom_call" | custom-call | flops 1610612736 | bytes 7864320 | tf_op jit(solution)/shard_map/project/pallas_call | solution.py:111
  151.3 4.0 %collective-permute-done.30.refs_1_ = bf16[3,4,32,1024]{3,2,1,0:T(8,128)(2,1)S(1)} collective-permute-done((bf16[3,4,32,1024]{3,2,1,0:T(8,128)(2,1)S(1)}, bf16[3,4,32,1024]{3,2,1,0:T(8,128)(2,1)S(1)}, u32[]{:S(2)}, u32[]{:S(2)}) %collective-permute-start.30) | collective-permute-done | bytes 786464 | tf_op jit(solution)/shard_map/ppermute | solution.py:333
  156.8 13.7 %collective-permute-start.23 = (bf16[4,32,1024]{2,1,0:T(8,128)(2,1)S(1)}, bf16[4,32,1024]{2,1,0:T(8,128)(2,1)}, u32[]{:S(2)}, u32[]{:S(2)}) collective-permute-start(bf16[4,32,1024]{2,1,0:T(8,128)(2,1)S(1)} %fusion.refs_0_), channel_id=1, source_target_pairs={{0,4},{2,6},{4,8},{6,10},{8,12},{10,14},{12,0},{14,2},{1,5},{3,7},... | collective-permute-start | bytes 786440 | tf_op jit(solution)/shard_map/ppermute | solution.py:330
  177.2 8.2 %collective-permute-done.24 = bf16[4,32,1024]{2,1,0:T(8,128)(2,1)} collective-permute-done((bf16[4,32,1024]{2,1,0:T(8,128)(2,1)S(1)}, bf16[4,32,1024]{2,1,0:T(8,128)(2,1)}, u32[]{:S(2)}, u32[]{:S(2)}) %collective-permute-start.24) | collective-permute-done | bytes 262176 | tf_op jit(solution)/shard_map/ppermute | solution.py:330
  191.3 18.0 %expert.6 = (bf16[4,2,32,2048]{3,2,1,0:T(8,128)(2,1)}, bf16[4,2,32,2048]{3,2,1,0:T(8,128)(2,1)}) custom-call(s32[8]{0:T(128)} %concatenate.29.order_ref, f32[2,256]{1,0:T(2,128)} %get-tuple-element.64.wt_ref, f32[1,4096]{1,0:T(1,128)} %bitcast.143, bf16[2,704,4096]{2,1,0:T(8,128)(2,1)} %bitcast.128, bf16[2,704,4096]{2,1,0:T(8,128)(2,1)} %bitcast.132, ...), custom_call_target="tpu_custom_call" | custom-call | flops 8858370048 | bytes 34603008 | tf_op jit(solution)/shard_map/expert/pallas_call | solution.py:252
  211.3 18.1 %expert.4 = (bf16[4,2,32,2048]{3,2,1,0:T(8,128)(2,1)}, bf16[4,2,32,2048]{3,2,1,0:T(8,128)(2,1)}, bf16[2,32,2048]{2,1,0:T(8,128)(2,1)}) custom-call(s32[8]{0:T(128)} %concatenate.29.order_ref, f32[2,256]{1,0:T(2,128)} %get-tuple-element.65.wt_ref, f32[1,4096]{1,0:T(1,128)} %bitcast.144, bf16[2,704,4096]{2,1,0:T(8,128)(2,1)} %bitcast.129, ...), custom_call_target="tpu_custom_call" | custom-call | flops 8858370048 | bytes 34603008 | tf_op jit(solution)/shard_map/expert/pallas_call | solution.py:252
  230.9 18.1 %expert.7 = (bf16[4,2,32,2048]{3,2,1,0:T(8,128)(2,1)}, bf16[4,2,32,2048]{3,2,1,0:T(8,128)(2,1)}) custom-call(s32[8]{0:T(128)} %concatenate.29.order_ref, f32[2,256]{1,0:T(2,128)} %get-tuple-element.66.wt_ref, f32[1,4096]{1,0:T(1,128)} %bitcast.145, bf16[2,704,4096]{2,1,0:T(8,128)(2,1)} %bitcast.130, bf16[2,704,4096]{2,1,0:T(8,128)(2,1)} %bitcast.134, ...), custom_call_target="tpu_custom_call" | custom-call | flops 8858370048 | bytes 34603008 | tf_op jit(solution)/shard_map/expert/pallas_call | solution.py:252
  251.1 18.2 %expert.5 = (bf16[4,2,32,2048]{3,2,1,0:T(8,128)(2,1)}, bf16[4,2,32,2048]{3,2,1,0:T(8,128)(2,1)}, bf16[2,32,2048]{2,1,0:T(8,128)(2,1)}) custom-call(s32[8]{0:T(128)} %concatenate.29.order_ref, f32[2,256]{1,0:T(2,128)} %get-tuple-element.67.wt_ref, f32[1,4096]{1,0:T(1,128)} %bitcast.146, bf16[2,704,4096]{2,1,0:T(8,128)(2,1)} %bitcast.131, ...), custom_call_target="tpu_custom_call" | custom-call | flops 8858370048 | bytes 34603008 | tf_op jit(solution)/shard_map/expert/pallas_call | solution.py:252
  270.6 5.1 %collective-permute-done.34.refs_0_ = bf16[4,2,32,2048]{3,2,1,0:T(8,128)(2,1)} collective-permute-done((bf16[4,2,32,2048]{3,2,1,0:T(8,128)(2,1)S(1)}, bf16[4,2,32,2048]{3,2,1,0:T(8,128)(2,1)}, u32[]{:S(2)}, u32[]{:S(2)}) %collective-permute-start.34) | collective-permute-done | bytes 1048608 | tf_op jit(solution)/shard_map/ppermute | solution.py:333
  279.2 8.4 %collective-permute-start.35 = (bf16[2,32,2048]{2,1,0:T(8,128)(2,1)}, bf16[2,32,2048]{2,1,0:T(8,128)(2,1)S(1)}, u32[]{:S(2)}, u32[]{:S(2)}) collective-permute-start(bf16[2,32,2048]{2,1,0:T(8,128)(2,1)} %get-tuple-element.38), channel_id=1, source_target_pairs={{0,4},{2,6},{4,8},{6,10},{8,12},{10,14},{12,0},{14,2},{1,5},{3,7},... | collective-permute-start | bytes 786440 | tf_op jit(solution)/shard_map/ppermute | solution.py:330
  291.5 6.1 %collective-permute-done.44.refs_0_ = bf16[4,2,32,2048]{3,2,1,0:T(8,128)(2,1)S(1)} collective-permute-done((bf16[4,2,32,2048]{3,2,1,0:T(8,128)(2,1)S(1)}, bf16[4,2,32,2048]{3,2,1,0:T(8,128)(2,1)S(1)}, u32[]{:S(2)}, u32[]{:S(2)}) %collective-permute-start.44) | collective-permute-done | bytes 1048608 | tf_op jit(solution)/shard_map/ppermute | solution.py:333
  302.1 8.4 %collective-permute-start.45 = (bf16[2,32,2048]{2,1,0:T(8,128)(2,1)}, bf16[2,32,2048]{2,1,0:T(8,128)(2,1)S(1)}, u32[]{:S(2)}, u32[]{:S(2)}) collective-permute-start(bf16[2,32,2048]{2,1,0:T(8,128)(2,1)} %get-tuple-element.46), channel_id=1, source_target_pairs={{0,4},{2,6},{4,8},{6,10},{8,12},{10,14},{12,0},{14,2},{1,5},{3,7},... | collective-permute-start | bytes 786440 | tf_op jit(solution)/shard_map/ppermute | solution.py:330
  313.7 7.2 %collective-permute-done.45 = bf16[2,32,2048]{2,1,0:T(8,128)(2,1)S(1)} collective-permute-done((bf16[2,32,2048]{2,1,0:T(8,128)(2,1)}, bf16[2,32,2048]{2,1,0:T(8,128)(2,1)S(1)}, u32[]{:S(2)}, u32[]{:S(2)}) %collective-permute-start.45) | collective-permute-done | bytes 262176 | tf_op jit(solution)/shard_map/ppermute | solution.py:330
  322.0 10.1 %collective-permute-done.36 = bf16[2,32,2048]{2,1,0:T(8,128)(2,1)S(1)} collective-permute-done((bf16[2,32,2048]{2,1,0:T(8,128)(2,1)S(1)}, bf16[2,32,2048]{2,1,0:T(8,128)(2,1)S(1)}, u32[]{:S(2)}, u32[]{:S(2)}) %collective-permute-start.36) | collective-permute-done | bytes 262176 | tf_op jit(solution)/shard_map/ppermute | solution.py:330
  332.3 4.4 %collective-permute-done.46 = bf16[2,32,2048]{2,1,0:T(8,128)(2,1)S(1)} collective-permute-done((bf16[2,32,2048]{2,1,0:T(8,128)(2,1)S(1)}, bf16[2,32,2048]{2,1,0:T(8,128)(2,1)S(1)}, u32[]{:S(2)}, u32[]{:S(2)}) %collective-permute-start.46) | collective-permute-done | bytes 262176 | tf_op jit(solution)/shard_map/ppermute | solution.py:330
  (211 shorter events, 95.0 us)
Async XLA Ops:
  3.8 92.4 %collective-permute-start.10 = (bf16[2048,512]{1,0:T(8,128)(2,1)}, bf16[2048,512]{1,0:T(8,128)(2,1)S(1)}, u32[]{:S(2)}, u32[]{:S(2)}) collective-permute-start(bf16[2048,512]{1,0:T(8,128)(2,1)} %slice.66), channel_id=1, source_target_pairs={{0,2},{2,0},{4,6},{6,4},{8,10},{10,8},{12,14},{14,12},{1,3},{3,1},... | collective-permute-start | bytes 6291464 | tf_op jit(solution)/shard_map/ppermute | solution.py:333
  21.7 55.5 %collective-permute-start.7 = (bf16[64,3072]{1,0:T(8,128)(2,1)}, bf16[64,3072]{1,0:T(8,128)(2,1)}, u32[]{:S(2)}, u32[]{:S(2)}) collective-permute-start(bf16[64,3072]{1,0:T(8,128)(2,1)} %attend.2.refs_0_), channel_id=1, source_target_pairs={{0,4},{2,6},{4,8},{6,10},{8,12},{10,14},{12,0},{14,2},{1,5},{3,7},... | collective-permute-start | bytes 1179656 | tf_op jit(solution)/shard_map/ppermute | solution.py:330
  23.3 68.3 %collective-permute-start.9 = (bf16[64,3072]{1,0:T(8,128)(2,1)}, bf16[64,3072]{1,0:T(8,128)(2,1)}, u32[]{:S(2)}, u32[]{:S(2)}) collective-permute-start(bf16[64,3072]{1,0:T(8,128)(2,1)} %attend.2.refs_0_), channel_id=1, source_target_pairs={{0,12},{2,14},{4,0},{6,2},{8,4},{10,6},{12,8},{14,10},{1,13},{3,15... | collective-permute-start | bytes 1179656 | tf_op jit(solution)/shard_map/ppermute | solution.py:330
  26.6 44.8 %collective-permute-start.11 = (bf16[512,512]{1,0:T(8,128)(2,1)S(1)}, bf16[512,512]{1,0:T(8,128)(2,1)S(1)}, u32[]{:S(2)}, u32[]{:S(2)}) collective-permute-start(bf16[512,512]{1,0:T(8,128)(2,1)S(1)} %constant_dynamic-slice_fusion.3), channel_id=1, source_target_pairs={{0,2},{2,0},{4,6},{6,4},{8,10},{10,8},{12,14},{14,12},{1,3},{3,1},... | collective-permute-start | bytes 1572872 | tf_op jit(solution)/shard_map/ppermute | solution.py:333
  27.6 36.5 %collective-permute-start = (f32[128,16]{0,1:T(8,128)}, f32[128,16]{0,1:T(8,128)}, u32[]{:S(2)}, u32[]{:S(2)}) collective-permute-start(f32[128,16]{0,1:T(8,128)} %get-tuple-element.69), channel_id=1, source_target_pairs={{0,2},{2,0},{4,6},{6,4},{8,10},{10,8},{12,14},{14,12},{1,3},{3,1},... | collective-permute-start | bytes 24584 | tf_op jit(solution)/shard_map/ppermute | solution.py:333
  71.4 24.1 %collective-permute-start.12 = (bf16[512,512]{1,0:T(8,128)(2,1)S(1)}, bf16[512,512]{1,0:T(8,128)(2,1)S(1)}, u32[]{:S(2)}, u32[]{:S(2)}) collective-permute-start(bf16[512,512]{1,0:T(8,128)(2,1)S(1)} %collective-permute-done.11.refs_5_), channel_id=1, source_target_pairs={{0,16},{16,0},{1,17},{17,1},{2,18},{18,2},{3,19},{19,3},{4,20},{20... | collective-permute-start | bytes 1572872 | tf_op jit(solution)/shard_map/ppermute | solution.py:337
  90.9 27.4 %collective-permute-start.19 = (bf16[64,3072]{1,0:T(8,128)(2,1)}, bf16[64,3072]{1,0:T(8,128)(2,1)}, u32[]{:S(2)}, u32[]{:S(2)}) collective-permute-start(bf16[64,3072]{1,0:T(8,128)(2,1)} %attend.3.refs_0_), channel_id=1, source_target_pairs={{0,4},{2,6},{4,8},{6,10},{8,12},{10,14},{12,0},{14,2},{1,5},{3,7},... | collective-permute-start | bytes 1179656 | tf_op jit(solution)/shard_map/ppermute | solution.py:330
  91.6 45.8 %collective-permute-start.21 = (bf16[64,3072]{1,0:T(8,128)(2,1)}, bf16[64,3072]{1,0:T(8,128)(2,1)S(1)}, u32[]{:S(2)}, u32[]{:S(2)}) collective-permute-start(bf16[64,3072]{1,0:T(8,128)(2,1)} %attend.3.refs_0_), channel_id=1, source_target_pairs={{0,12},{2,14},{4,0},{6,2},{8,4},{10,6},{12,8},{14,10},{1,13},{3,15... | collective-permute-start | bytes 1179656 | tf_op jit(solution)/shard_map/ppermute | solution.py:330
  118.2 24.0 %collective-permute-start.20 = (bf16[64,3072]{1,0:T(8,128)(2,1)}, bf16[64,3072]{1,0:T(8,128)(2,1)S(1)}, u32[]{:S(2)}, u32[]{:S(2)}) collective-permute-start(bf16[64,3072]{1,0:T(8,128)(2,1)} %collective-permute-done.19.refs_1_), channel_id=1, source_target_pairs={{0,4},{2,6},{4,8},{6,10},{8,12},{10,14},{12,0},{14,2},{1,5},{3,7},... | collective-permute-start | bytes 1179656 | tf_op jit(solution)/shard_map/ppermute | solution.py:330
  149.7 23.2 %collective-permute-start.29 = (bf16[4,32,1024]{2,1,0:T(8,128)(2,1)S(1)}, bf16[4,32,1024]{2,1,0:T(8,128)(2,1)}, u32[]{:S(2)}, u32[]{:S(2)}) collective-permute-start(bf16[4,32,1024]{2,1,0:T(8,128)(2,1)S(1)} %fusion.1.refs_0_), channel_id=1, source_target_pairs={{0,2},{2,0},{4,6},{6,4},{8,10},{10,8},{12,14},{14,12},{1,3},{3,1},... | collective-permute-start | bytes 786440 | tf_op jit(solution)/shard_map/ppermute | solution.py:333
  155.2 34.5 %collective-permute-start.32 = (bf16[3,4,32,1024]{3,2,1,0:T(8,128)(2,1)S(1)}, bf16[3,4,32,1024]{3,2,1,0:T(8,128)(2,1)S(1)}, u32[]{:S(2)}, u32[]{:S(2)}) collective-permute-start(bf16[3,4,32,1024]{3,2,1,0:T(8,128)(2,1)S(1)} %collective-permute-done.30.refs_1_), channel_id=1, source_target_pairs={{0,1},{1,0},{2,3},{3,2},{4,5},{5,4},{6,7},{7,6},{8,9},{9,8},{10,11... | collective-permute-start | bytes 2359304 | tf_op jit(solution)/shard_map/ppermute | solution.py:335
  177.2 32.2 %collective-permute-start.17 = (bf16[4,32,1024]{2,1,0:T(8,128)(2,1)S(1)}, bf16[4,32,1024]{2,1,0:T(8,128)(2,1)S(1)}, u32[]{:S(2)}, u32[]{:S(2)}) collective-permute-start(bf16[4,32,1024]{2,1,0:T(8,128)(2,1)S(1)} %fusion.1.refs_0_), channel_id=1, source_target_pairs={{0,1},{1,0},{2,3},{3,2},{4,5},{5,4},{6,7},{7,6},{8,9},{9,8},{10,11... | collective-permute-start | bytes 786440 | tf_op jit(solution)/shard_map/ppermute | solution.py:335
  185.4 24.1 %collective-permute-start.39 = (bf16[4,32,1024]{2,1,0:T(8,128)(2,1)S(1)}, bf16[4,32,1024]{2,1,0:T(8,128)(2,1)S(1)}, u32[]{:S(2)}, u32[]{:S(2)}) collective-permute-start(bf16[4,32,1024]{2,1,0:T(8,128)(2,1)S(1)} %fusion.refs_0_), channel_id=1, source_target_pairs={{0,2},{2,0},{4,6},{6,4},{8,10},{10,8},{12,14},{14,12},{1,3},{3,1},... | collective-permute-start | bytes 786440 | tf_op jit(solution)/shard_map/ppermute | solution.py:333
  188.0 63.1 %collective-permute-start.26 = (bf16[4,32,1024]{2,1,0:T(8,128)(2,1)S(1)}, bf16[4,32,1024]{2,1,0:T(8,128)(2,1)}, u32[]{:S(2)}, u32[]{:S(2)}) collective-permute-start(bf16[4,32,1024]{2,1,0:T(8,128)(2,1)S(1)} %fusion.refs_0_), channel_id=1, source_target_pairs={{0,1},{1,0},{2,3},{3,2},{4,5},{5,4},{6,7},{7,6},{8,9},{9,8},{10,11... | collective-permute-start | bytes 786440 | tf_op jit(solution)/shard_map/ppermute | solution.py:335
  189.2 21.2 %collective-permute-start.18 = (bf16[3,4,32,1024]{3,2,1,0:T(8,128)(2,1)S(1)}, bf16[3,4,32,1024]{3,2,1,0:T(8,128)(2,1)S(1)}, u32[]{:S(2)}, u32[]{:S(2)}) collective-permute-start(bf16[3,4,32,1024]{3,2,1,0:T(8,128)(2,1)S(1)} %pad_maximum_fusion.refs_1_), channel_id=1, source_target_pairs={{0,1},{1,0},{2,3},{3,2},{4,5},{5,4},{6,7},{7,6},{8,9},{9,8},{10,11... | collective-permute-start | bytes 2359304 | tf_op jit(solution)/shard_map/ppermute | solution.py:335
  209.4 41.7 %collective-permute-start.27 = (bf16[3,4,32,1024]{3,2,1,0:T(8,128)(2,1)S(1)}, bf16[3,4,32,1024]{3,2,1,0:T(8,128)(2,1)}, u32[]{:S(2)}, u32[]{:S(2)}) collective-permute-start(bf16[3,4,32,1024]{3,2,1,0:T(8,128)(2,1)S(1)} %pad_maximum_fusion.1.refs_1_), channel_id=1, source_target_pairs={{0,1},{1,0},{2,3},{3,2},{4,5},{5,4},{6,7},{7,6},{8,9},{9,8},{10,11... | collective-permute-start | bytes 2359304 | tf_op jit(solution)/shard_map/ppermute | solution.py:335
  210.4 38.7 %collective-permute-start.33 = (bf16[4,2,32,2048]{3,2,1,0:T(8,128)(2,1)}, bf16[4,2,32,2048]{3,2,1,0:T(8,128)(2,1)S(1)}, u32[]{:S(2)}, u32[]{:S(2)}) collective-permute-start(bf16[4,2,32,2048]{3,2,1,0:T(8,128)(2,1)} %get-tuple-element.35), channel_id=1, source_target_pairs={{0,1},{1,0},{2,3},{3,2},{4,5},{5,4},{6,7},{7,6},{8,9},{9,8},{10,11... | collective-permute-start | bytes 3145736 | tf_op jit(solution)/shard_map/ppermute | solution.py:335
  229.5 41.1 %collective-permute-start.28 = (bf16[4,2,32,2048]{3,2,1,0:T(8,128)(2,1)}, bf16[4,2,32,2048]{3,2,1,0:T(8,128)(2,1)}, u32[]{:S(2)}, u32[]{:S(2)}) collective-permute-start(bf16[4,2,32,2048]{3,2,1,0:T(8,128)(2,1)} %get-tuple-element.33), channel_id=1, source_target_pairs={{0,1},{1,0},{2,3},{3,2},{4,5},{5,4},{6,7},{7,6},{8,9},{9,8},{10,11... | collective-permute-start | bytes 3145736 | tf_op jit(solution)/shard_map/ppermute | solution.py:335
  249.5 26.2 %collective-permute-start.34 = (bf16[4,2,32,2048]{3,2,1,0:T(8,128)(2,1)S(1)}, bf16[4,2,32,2048]{3,2,1,0:T(8,128)(2,1)}, u32[]{:S(2)}, u32[]{:S(2)}) collective-permute-start(bf16[4,2,32,2048]{3,2,1,0:T(8,128)(2,1)S(1)} %add_convert_fusion.1), channel_id=1, source_target_pairs={{0,2},{2,0},{4,6},{6,4},{8,10},{10,8},{12,14},{14,12},{1,3},{3,1},... | collective-permute-start | bytes 3145736 | tf_op jit(solution)/shard_map/ppermute | solution.py:333
  269.3 22.1 %collective-permute-start.38 = (bf16[4,2,32,2048]{3,2,1,0:T(8,128)(2,1)}, bf16[4,2,32,2048]{3,2,1,0:T(8,128)(2,1)}, u32[]{:S(2)}, u32[]{:S(2)}) collective-permute-start(bf16[4,2,32,2048]{3,2,1,0:T(8,128)(2,1)} %get-tuple-element.41), channel_id=1, source_target_pairs={{0,1},{1,0},{2,3},{3,2},{4,5},{5,4},{6,7},{7,6},{8,9},{9,8},{10,11... | collective-permute-start | bytes 3145736 | tf_op jit(solution)/shard_map/ppermute | solution.py:335
  270.0 27.6 %collective-permute-start.44 = (bf16[4,2,32,2048]{3,2,1,0:T(8,128)(2,1)S(1)}, bf16[4,2,32,2048]{3,2,1,0:T(8,128)(2,1)S(1)}, u32[]{:S(2)}, u32[]{:S(2)}) collective-permute-start(bf16[4,2,32,2048]{3,2,1,0:T(8,128)(2,1)S(1)} %add_convert_fusion), channel_id=1, source_target_pairs={{0,2},{2,0},{4,6},{6,4},{8,10},{10,8},{12,14},{14,12},{1,3},{3,1},... | collective-permute-start | bytes 3145736 | tf_op jit(solution)/shard_map/ppermute | solution.py:333
  279.2 34.3 %collective-permute-start.35 = (bf16[2,32,2048]{2,1,0:T(8,128)(2,1)}, bf16[2,32,2048]{2,1,0:T(8,128)(2,1)S(1)}, u32[]{:S(2)}, u32[]{:S(2)}) collective-permute-start(bf16[2,32,2048]{2,1,0:T(8,128)(2,1)} %get-tuple-element.38), channel_id=1, source_target_pairs={{0,4},{2,6},{4,8},{6,10},{8,12},{10,14},{12,0},{14,2},{1,5},{3,7},... | collective-permute-start | bytes 786440 | tf_op jit(solution)/shard_map/ppermute | solution.py:330
  288.5 33.5 %collective-permute-start.37 = (bf16[2,32,2048]{2,1,0:T(8,128)(2,1)}, bf16[2,32,2048]{2,1,0:T(8,128)(2,1)S(1)}, u32[]{:S(2)}, u32[]{:S(2)}) collective-permute-start(bf16[2,32,2048]{2,1,0:T(8,128)(2,1)} %get-tuple-element.39), channel_id=1, source_target_pairs={{0,12},{2,14},{4,0},{6,2},{8,4},{10,6},{12,8},{14,10},{1,13},{3,15... | collective-permute-start | bytes 786440 | tf_op jit(solution)/shard_map/ppermute | solution.py:330
  310.6 21.7 %collective-permute-start.47 = (bf16[2,32,2048]{2,1,0:T(8,128)(2,1)}, bf16[2,32,2048]{2,1,0:T(8,128)(2,1)S(1)}, u32[]{:S(2)}, u32[]{:S(2)}) collective-permute-start(bf16[2,32,2048]{2,1,0:T(8,128)(2,1)} %get-tuple-element.47), channel_id=1, source_target_pairs={{0,12},{2,14},{4,0},{6,2},{8,4},{10,6},{12,8},{14,10},{1,13},{3,15... | collective-permute-start | bytes 786440 | tf_op jit(solution)/shard_map/ppermute | solution.py:330
  (58 other events, 925.6 us)
where the time goes:
time: 338 us
  Pallas kernels  117 us (35%)
  waiting for transfers between devices  113 us (33%)
  starting transfers between devices  79.2 us (23%)
  local copies, waits for them, and re-layouts  17.9 us (5%)
  other arithmetic  9.09 us (3%)
    ppermute x24, waiting for transfers between devices, shift(): return lax.ppermute(x, 'dev', pairs)  80.3 us
    pallas_call x4, Pallas kernels, expert(): pl.pallas_call(functools.partial(expert_body, nz=nz, eps=1e-05, show=show...  72.4 us
    ppermute x24, starting transfers between devices, shift(): return lax.ppermute(x, 'dev', pairs)  61.7 us
    ppermute x9, waiting for transfers between devices, across(): lax.ppermute(x, 'dev', [(a * ny + b, a * ny + (b + 1) % ny) for a in rang...  33.1 us
    pallas_call x2, Pallas kernels, attend(): pl.pallas_call(functools.partial(attend_body, seq=seq, kv=kv, heads=heads...  24.2 us
    ppermute x9, starting transfers between devices, across(): lax.ppermute(x, 'dev', [(a * ny + b, a * ny + (b + 1) % ny) for a in rang...  13.5 us
    pallas_call x2, Pallas kernels, project(): pl.pallas_call(functools.partial(project_body, nz=nz), out_shape=(jax.Sha...  13.1 us
    pallas_call x2, Pallas kernels, settle(): pl.pallas_call(functools.partial(settle_body, nz=nz, adds=len(extra), spr...  7.03 us
  transfers between devices with their start and end apart: 48, of which 19 were waited for; matrix products, arithmetic and copies ran while one was open for 6% of the time, Pallas kernels for 35%

commit v1 on v0

--- a/solution.py
+++ b/solution.py
@@ -24,11 +24,16 @@
     n = kb * kv
     r = lax.broadcasted_iota(jnp.int32, (n, n), 0); cc = lax.broadcasted_iota(jnp.int32, (n, n), 1)
     perm = (cc == (r % kb) * kv + r // kb).astype(jnp.bfloat16)
-    for b in range(count // kb):
+
+    def sort(b, _):
+        at, to = pl.ds(pl.multiple_of(b * n, n), n), pl.ds(pl.multiple_of(b * kb, kb), kb)
         for src, dst in ((k_ref, ks), (v_ref, vs)):
-            t = jnp.dot(perm, src[b * n:(b + 1) * n], preferred_element_type=jnp.float32).astype(jnp.bfloat16)
+            t = jnp.dot(perm, src[at], preferred_element_type=jnp.float32).astype(jnp.bfloat16)
             for h in range(kv):
-                dst[h, b * kb:(b + 1) * kb] = t[h * kb:(h + 1) * kb]
+                dst[h, to] = t[h * kb : (h + 1) * kb]
+        return 0
+
+    lax.fori_loop(0, count // kb, sort, 0, unroll=2)
     valid = lax.broadcasted_iota(jnp.int32, (1, count), 1) < length
     wide = step * hd
     row = lax.broadcasted_iota(jnp.int32, (step * tok, tok), 0) % tok
@@ -69,7 +74,7 @@
         grid_spec=pltpu.PrefetchScalarGridSpec(num_scalar_prefetch=1, grid=(1,),
             in_specs=[whole(q), kspec, kspec, whole(fk), whole(fv)], out_specs=whole(q),
             scratch_shapes=[pltpu.VMEM((kv, rows // kv, hd), jnp.bfloat16)] * 2),
-        compiler_params=pltpu.CompilerParams(vmem_limit_bytes=VMEM),
+        compiler_params=pltpu.CompilerParams(vmem_limit_bytes=VMEM // 2),
         cost_estimate=cost(4 * tok * wide * (rows // kv), 4 * rows * hd, tok * wide // hd * (rows // kv)), name="attend")(lengths, q, keys, values, fk, fv)
 
 
@@ -118,7 +123,7 @@
             out_specs=[pl.BlockSpec(shape, lambda i, o: (0, 0, 0))] * 2,
             scratch_shapes=[pltpu.VMEM((nz * rows, depth), jnp.bfloat16)],
         ),
-        compiler_params=pltpu.CompilerParams(vmem_limit_bytes=VMEM),
+        compiler_params=pltpu.CompilerParams(vmem_limit_bytes=VMEM * 2 // 3),
         cost_estimate=cost(2 * nz * rows * depth * cols, 2 * (nz * rows * depth + depth * cols)),
         name="project",
     )(order, w, *slots, *pieces)
@@ -129,9 +134,9 @@
     theirs_ref, ours_ref, refs = refs[0], refs[1], refs[2:]
     if show:
         hid_ref, refs = refs[0], refs[1:]
-    wbuf, dbuf, xs, res, act_t, acts, r_t, ss, first_sem, block_sem, down_sem = refs
+    pbuf, wbuf, dbuf, xs, res, act_t, acts, r_t, ss, row_sem, first_sem, block_sem, down_sem = refs
     head, me = order_ref[nz], order_ref[nz + 3]
-    _, part, cw = p[0].shape
+    part, cw = pbuf.shape[3:]
     rows = 2 * nz * part
     half = nz // 2
     experts, ff, _ = gate_hbm.shape
@@ -139,6 +144,10 @@
     span = lambda c: pl.ds(pl.multiple_of(c * cw, cw), cw)
     sources = (gate_hbm, up_hbm)
 
+    def gathered(j):
+        both = (p[0], p[2]) if isinstance(j, int) and j == 0 else (p[1].at[j - 1], p[3].at[j - 1])
+        return [pltpu.make_async_copy(src, pbuf.at[j, k], row_sem.at[k, j]) for k, src in enumerate(both)]
+
     def first(j):
         at = span(order_ref[j])
         return [
@@ -166,44 +175,40 @@
             c.wait()
 
     for j in range(nz):
+        start(gathered(j))
         start(first(j))
     if experts > 1:
         start(block(1))
     down_half(0).start()
 
-    def chunk(j, own, other, begin):
+    def chunk(j, _):
         c = order_ref[j]
         at = span(c)
-        v = jnp.concatenate([own[...], other[...]], 0).reshape(rows, cw).astype(jnp.float32)
-        xs[:, at] = (v * gain_ref[:, at]).astype(jnp.bfloat16)
+        for k in range(2):
+            pltpu.make_async_copy(p[0], pbuf.at[j, k], row_sem.at[k, j]).wait()
+        v = pbuf[j].reshape(rows, cw).astype(jnp.float32)
+        x = (v * gain_ref[:, at]).astype(jnp.bfloat16)
+        xs[:, at] = x
         wait(first(j))
-
-        def product(i, _):
-            out = lax.dot_general(wbuf[0, i, :, at], xs[:, at], LAST, preferred_element_type=jnp.float32)
-            res[i] = out if begin else res[i] + out
-            return 0
-
-        lax.fori_loop(0, 2, product, 0)
+        for i in range(2):
+            out = lax.dot_general(wbuf[0, i, :, at], x, LAST, preferred_element_type=jnp.float32)
+            res[i] = jnp.where(j > 0, res[i], 0.0) + out
         v = v * v
         total = v[:, :128]
         for i in range(128, cw, 128):
             total = total + v[:, i : i + 128]
-        ss[...] = total if begin else ss[...] + total
+        ss[...] = jnp.where(j > 0, ss[...], 0.0) + total
         if show:
 
             @pl.when(c // half == head)
             def _():
                 to = span(c % half)
-                hid_ref[0, :, to] = own[me]
-                hid_ref[1, :, to] = other[me]
-
-    chunk(0, p[0], p[2], True)
-
-    def later(j, _):
-        chunk(j, p[1].at[j - 1], p[3].at[j - 1], False)
+                hid_ref[head, :, to] = pbuf[j, 0, me]
+                hid_ref[1 - head, :, to] = pbuf[j, 1, me]
+
         return 0
 
-    lax.fori_loop(1, nz, later, 0)
+    lax.fori_loop(0, nz, chunk, 0)
     r_t[...] = lax.rsqrt(jnp.sum(ss[...].T, axis=0, keepdims=True) / (nz * cw) + eps)
 
     def activate(e):
@@ -216,11 +221,8 @@
     for e in range(1, experts):
         wait(block(e))
 
-        def product(i, _, e=e):
+        for i in range(2):
             res[i] = lax.dot_general(wbuf[e % 2, i], xs[...], LAST, preferred_element_type=jnp.float32)
-            return 0
-
-        lax.fori_loop(0, 2, product, 0)
         if e + 1 < experts:
             start(block(e + 1))
         activate(e)
@@ -248,13 +250,16 @@
     shapes = [out, out]
     if show:
         shapes.append(jax.ShapeDtypeStruct((2, part, nz // 2 * cw), jnp.bfloat16))
-    vmem, hbm = pl.BlockSpec(memory_space=pltpu.VMEM), pl.BlockSpec(memory_space=pl.ANY)
+    held = 4 * depth * ff * (2 * min(2, experts)) // 2 + 4 * experts * ff * cols + 4 * rows * depth + 8 * ff * rows
+    held += 4 * experts * ff * rows + 4 * rows * cols
+    vmem, hbm = pl.BlockSpec(memory_space=pltpu.VMEM), pl.BlockSpec(memory_space=pltpu.HBM)
     return pl.pallas_call(
         functools.partial(expert_body, nz=nz, eps=1e-5, show=show),
         out_shape=shapes,
-        in_specs=[pl.BlockSpec(memory_space=pltpu.SMEM), vmem, vmem, hbm, hbm, hbm] + [vmem] * 4,
+        in_specs=[pl.BlockSpec(memory_space=pltpu.SMEM), vmem, vmem, hbm, hbm, hbm] + [hbm] * 4,
         out_specs=[vmem] * len(shapes),
         scratch_shapes=[
+            pltpu.VMEM((nz, 2, nz, part, cw), jnp.bfloat16),
             pltpu.VMEM((min(2, experts), 2, ff, depth), jnp.bfloat16),
             pltpu.VMEM((2, experts, ff, cols), jnp.bfloat16),
             pltpu.VMEM((rows, depth), jnp.bfloat16),
@@ -264,10 +269,11 @@
             pltpu.VMEM((1, rows), jnp.float32),
             pltpu.VMEM((rows, 128), jnp.float32),
             pltpu.SemaphoreType.DMA((2, nz)),
+            pltpu.SemaphoreType.DMA((2, nz)),
             pltpu.SemaphoreType.DMA((2, 2)),
             pltpu.SemaphoreType.DMA((2,)),
         ],
-        compiler_params=pltpu.CompilerParams(vmem_limit_bytes=VMEM),
+        compiler_params=pltpu.CompilerParams(vmem_limit_bytes=min(VMEM, held + (8 << 20))),
         cost_estimate=cost(6 * rows * depth * ff * experts, 6 * depth * ff * experts),
         name="expert",
     )(order, wt, gain, gate_t, up_t, down_w, *p)
@@ -306,7 +312,7 @@
         grid_spec=pltpu.PrefetchScalarGridSpec(
             num_scalar_prefetch=1, grid=(steps,), in_specs=[block] * (2 + len(extra)), out_specs=specs
         ),
-        compiler_params=pltpu.CompilerParams(vmem_limit_bytes=VMEM),
+        compiler_params=pltpu.CompilerParams(vmem_limit_bytes=VMEM // 2),
         cost_estimate=cost(4 * ours.size, 2 * ours.size * (3 + len(extra))),
         name="settle",
     )(order, ours, theirs, *extra)
@@ -433,17 +439,24 @@
     def finish(s):
         extra = (summed[s, 1],) if ny > 1 else ()
         terms = settle(*summed[s, 0], order, extra, True)
-        moved = {}
-        for step, count in ((1, nz // 2), (-1, nz - 1 - nz // 2)):
-            for i, k in enumerate(range(count, 0, -1)):
-                term = terms[step * k]
-                if i:
-                    term = (term.astype(f32) + moved[step].astype(f32)).astype(bf16)
-                moved[step] = shift(term, step)
+        got = []
+        if s < seqs - 1:
+            for k in range(1, nz):
+                got.append(shift(terms[k], k))
+        else:
+            for step, count in ((1, nz // 2), (-1, nz - 1 - nz // 2)):
+                moved = None
+                for i, k in enumerate(range(count, 0, -1)):
+                    term = terms[step * k]
+                    if i:
+                        term = (term.astype(f32) + moved.astype(f32)).astype(bf16)
+                    moved = shift(term, step)
+                got.append(moved)
         final = terms[0].astype(f32)
-        for got in moved.values():
-            final = final + got.astype(f32)
-        moe_parts[s] = final.astype(bf16)
+        for term in got:
+            final = final + term.astype(f32)
+        final = final.astype(bf16)
+        moe_parts[s] = jnp.where(head == 0, final, final[::-1])
 
     if ny == 1:
         for s in range(seqs):
@@ -459,8 +472,10 @@
             if not first_plane:
                 other_plane(s)
             finish(s)
-    place = lambda parts: jnp.stack([jnp.where(head == 0, p, p[::-1]) for p in parts]).reshape(tok, -1)
-    return place(hidden_parts), place(moe_parts)
+    place = lambda parts: jnp.concatenate([p.reshape(resp, -1) for p in parts])
+    hidden_out = place(hidden_parts)
+    moe_out = place(moe_parts)
+    return hidden_out, moe_out
 
 
 def solution(mesh):

time: 338 us -> 377 us (1.12); the launches traced: 338 us -> 373 us
  waiting for transfers between devices: 113 us -> 168 us
  Pallas kernels: 117 us -> 97.1 us
  starting transfers between devices: 79.2 us -> 64.9 us
  local copies, waits for them, and re-layouts: 17.9 us -> 30.8 us
    ppermute x9, waiting for transfers between devices: 33.1 us -> 83.1 us  [across(): lax.ppermute(x, 'dev', [(a * ny + b, a * ny + (b + 1) % ny) for a in rang...]
    ppermute x24, starting transfers between devices: 61.7 us -> 51.9 us  [shift(): return lax.ppermute(x, 'dev', pairs)]
    unnamed x74 -> x60, local copies, waits for them, and re-layouts: 5.44 us -> 14.9 us
    pallas_call x4, Pallas kernels: 72.4 us -> 65.4 us  [expert(): pl.pallas_call(functools.partial(expert_body, nz=nz, eps=1e-05, show=show...]
    pallas_call x2, Pallas kernels: 13.1 us -> 8.14 us  [project(): pl.pallas_call(functools.partial(project_body, nz=nz), out_shape=(jax.Sha...]
    ppermute x9, starting transfers between devices: 13.5 us -> 8.94 us  [across(): lax.ppermute(x, 'dev', [(a * ny + b, a * ny + (b + 1) % ny) for a in rang...]
    pallas_call x2, Pallas kernels: 7.03 us -> 2.53 us  [settle(): pl.pallas_call(functools.partial(settle_body, nz=nz, adds=len(extra), spr...]
    ppermute x24, waiting for transfers between devices: 80.3 us -> 84.5 us  [shift(): return lax.ppermute(x, 'dev', pairs)]
  transfers between devices with their start and end apart: 48 -> 48, of which waited for: 19 -> 22; matrix products, arithmetic and copies ran while one was open for 6% -> 8% of each run, Pallas kernels for 35% -> 26%
where the time goes in v1:
time: 377 us; the launch traced here: 373 us
  waiting for transfers between devices  168 us (45%)
  Pallas kernels  97.1 us (26%)
  starting transfers between devices  64.9 us (17%)
  local copies, waits for them, and re-layouts  30.8 us (8%)
  other arithmetic  11 us (3%)
    ppermute x24, waiting for transfers between devices, shift(): return lax.ppermute(x, 'dev', pairs)  84.5 us
    ppermute x9, waiting for transfers between devices, across(): lax.ppermute(x, 'dev', [(a * ny + b, a * ny + (b + 1) % ny) for a in rang...  83.1 us
    pallas_call x4, Pallas kernels, expert(): pl.pallas_call(functools.partial(expert_body, nz=nz, eps=1e-05, show=show...  65.4 us
    ppermute x24, starting transfers between devices, shift(): return lax.ppermute(x, 'dev', pairs)  51.9 us
    pallas_call x2, Pallas kernels, attend(): pl.pallas_call(functools.partial(attend_body, seq=seq, kv=kv, heads=heads...  21 us
    unnamed x60, local copies, waits for them, and re-layouts  14.9 us
    ppermute x9, starting transfers between devices, across(): lax.ppermute(x, 'dev', [(a * ny + b, a * ny + (b + 1) % ny) for a in rang...  8.94 us
    pallas_call x2, Pallas kernels, project(): pl.pallas_call(functools.partial(project_body, nz=nz), out_shape=(jax.Sha...  8.14 us
  transfers between devices with their start and end apart: 48, of which 22 were waited for; matrix products, arithmetic and copies ran while one was open for 8% of the time, Pallas kernels for 26%

profile of v1, /device:TPU:0, one launch (start us, length us, event | category | flops | bytes accessed | tf_op | source)
XLA Modules:
  0.0 372.6 jit_solution(313144111268284430)
XLA Ops:
  14.9 10.5 %attend.2.refs_0_ = bf16[64,3072]{1,0:T(8,128)(2,1)S(1)} custom-call(s32[2]{0:T(128)S(1)} %copy-done.14, bf16[64,3072]{1,0:T(8,128)(2,1)S(1)} %bitcast.123, bf16[2,4096,128]{2,1,0:T(8,128)(2,1)S(1)} %bitcast.130, bf16[2,4096,128]{2,1,0:T(8,128)(2,1)S(1)} %bitcast.132, bf16[64,256]{1,0:T(8,128)(2,1)S(1)} %get-tuple-element.73.nk_ref, ...), custom_call_target="tpu_custom_call" | custom-call | flops 1610612736 | bytes 2097152 | tf_op jit(solution)/shard_map/attend/pallas_call | solution.py:71
  42.1 10.5 %attend.3.refs_0_ = bf16[64,3072]{1,0:T(8,128)(2,1)S(1)} custom-call(s32[2]{0:T(128)S(1)} %copy-done.14, bf16[64,3072]{1,0:T(8,128)(2,1)S(1)} %bitcast.122, bf16[2,4096,128]{2,1,0:T(8,128)(2,1)S(1)} %bitcast.131, bf16[2,4096,128]{2,1,0:T(8,128)(2,1)S(1)} %bitcast.133, bf16[64,256]{1,0:T(8,128)(2,1)S(1)} %copy-done.9, bf16[64,256]{1,0:T(8,128)(2,1)S(1)} %copy-done.8), custom_call_target="tpu_custom_call" | custom-call | flops 1610612736 | bytes 2097152 | tf_op jit(solution)/shard_map/attend/pallas_call | solution.py:71
  55.3 20.4 %collective-permute-done = f32[128,16]{0,1:T(8,128)} collective-permute-done((f32[128,16]{0,1:T(8,128)}, f32[128,16]{0,1:T(8,128)}, u32[]{:S(2)}, u32[]{:S(2)}) %collective-permute-start) | collective-permute-done | bytes 8224 | tf_op jit(solution)/shard_map/ppermute | solution.py:339
  82.5 4.0 %collective-permute-done.2 = f32[2,128,16]{1,2,0:T(8,128)S(1)} collective-permute-done((f32[2,128,16]{1,2,0:T(8,128)S(1)}, f32[2,128,16]{1,2,0:T(8,128)S(1)}, u32[]{:S(2)}, u32[]{:S(2)}) %collective-permute-start.2) | collective-permute-done | bytes 16416 | tf_op jit(solution)/shard_map/ppermute | solution.py:336
  99.7 7.2 %collective-permute-start.9 = (bf16[64,3072]{1,0:T(8,128)(2,1)S(1)}, bf16[64,3072]{1,0:T(8,128)(2,1)S(1)}, u32[]{:S(2)}, u32[]{:S(2)}) collective-permute-start(bf16[64,3072]{1,0:T(8,128)(2,1)S(1)} %attend.2.refs_0_), channel_id=1, source_target_pairs={{0,12},{2,14},{4,0},{6,2},{8,4},{10,6},{12,8},{14,10},{1,13},{3,15... | collective-permute-start | bytes 1179656 | tf_op jit(solution)/shard_map/ppermute | solution.py:336
  116.5 4.3 %collective-permute-start.21 = (bf16[64,3072]{1,0:T(8,128)(2,1)}, bf16[64,3072]{1,0:T(8,128)(2,1)S(1)}, u32[]{:S(2)}, u32[]{:S(2)}) collective-permute-start(bf16[64,3072]{1,0:T(8,128)(2,1)} %copy-done.4), channel_id=1, source_target_pairs={{0,12},{2,14},{4,0},{6,2},{8,4},{10,6},{12,8},{14,10},{1,13},{3,15... | collective-permute-start | bytes 1179656 | tf_op jit(solution)/shard_map/ppermute | solution.py:336
  120.8 4.2 %collective-permute-done.19.refs_1_ = bf16[64,3072]{1,0:T(8,128)(2,1)S(1)} collective-permute-done((bf16[64,3072]{1,0:T(8,128)(2,1)}, bf16[64,3072]{1,0:T(8,128)(2,1)S(1)}, u32[]{:S(2)}, u32[]{:S(2)}) %collective-permute-start.19) | collective-permute-done | bytes 393248 | tf_op jit(solution)/shard_map/ppermute | solution.py:336
  131.4 4.1 %project.2 = (f32[4,32,1024]{2,1,0:T(8,128)S(1)}, bf16[4,32,1024]{2,1,0:T(8,128)(2,1)S(1)}) custom-call(s32[8]{0:T(128)S(1)} %concatenate.35.order_ref, bf16[3072,512]{1,0:T(8,128)(2,1)S(1)} %copy-done, bf16[64,3072]{1,0:T(8,128)(2,1)S(1)} %attend.2.refs_0_, bf16[64,3072]{1,0:T(8,128)(2,1)} %collective-permute-done.7.refs_1_, ...), custom_call_target="tpu_custom_call" | custom-call | flops 1610612736 | bytes 7864320 | tf_op jit(solution)/shard_map/project/pallas_call | solution.py:116
  135.7 4.2 %collective-permute-done.20.refs_2_ = bf16[64,3072]{1,0:T(8,128)(2,1)S(1)} collective-permute-done((bf16[64,3072]{1,0:T(8,128)(2,1)S(1)}, bf16[64,3072]{1,0:T(8,128)(2,1)S(1)}, u32[]{:S(2)}, u32[]{:S(2)}) %collective-permute-start.20) | collective-permute-done | bytes 393248 | tf_op jit(solution)/shard_map/ppermute | solution.py:336
  158.9 8.5 %collective-permute-done.15 = bf16[4,32,1024]{2,1,0:T(8,128)(2,1)S(1)} collective-permute-done((bf16[4,32,1024]{2,1,0:T(8,128)(2,1)S(1)}, bf16[4,32,1024]{2,1,0:T(8,128)(2,1)S(1)}, u32[]{:S(2)}, u32[]{:S(2)}) %collective-permute-start.15) | collective-permute-done | bytes 262176 | tf_op jit(solution)/shard_map/ppermute | solution.py:336
  167.6 5.5 %collective-permute-done.23 = bf16[4,32,1024]{2,1,0:T(8,128)(2,1)S(1)} collective-permute-done((bf16[4,32,1024]{2,1,0:T(8,128)(2,1)S(1)}, bf16[4,32,1024]{2,1,0:T(8,128)(2,1)S(1)}, u32[]{:S(2)}, u32[]{:S(2)}) %collective-permute-start.23) | collective-permute-done | bytes 262176 | tf_op jit(solution)/shard_map/ppermute | solution.py:336
  173.1 16.2 %collective-permute-done.24 = bf16[4,32,1024]{2,1,0:T(8,128)(2,1)S(1)} collective-permute-done((bf16[4,32,1024]{2,1,0:T(8,128)(2,1)S(1)}, bf16[4,32,1024]{2,1,0:T(8,128)(2,1)S(1)}, u32[]{:S(2)}, u32[]{:S(2)}) %collective-permute-start.24) | collective-permute-done | bytes 262176 | tf_op jit(solution)/shard_map/ppermute | solution.py:336
  192.7 22.8 %collective-permute-done.39.refs_0_ = bf16[4,32,1024]{2,1,0:T(8,128)(2,1)S(1)} collective-permute-done((bf16[4,32,1024]{2,1,0:T(8,128)(2,1)S(1)}, bf16[4,32,1024]{2,1,0:T(8,128)(2,1)S(1)}, u32[]{:S(2)}, u32[]{:S(2)}) %collective-permute-start.39) | collective-permute-done | bytes 262176 | tf_op jit(solution)/shard_map/ppermute | solution.py:339
  216.5 17.1 %expert.4 = (bf16[4,2,32,2048]{3,2,1,0:T(8,128)(2,1)S(1)}, bf16[4,2,32,2048]{3,2,1,0:T(8,128)(2,1)}, bf16[2,32,2048]{2,1,0:T(8,128)(2,1)S(1)}) custom-call(s32[8]{0:T(128)S(1)} %concatenate.35.order_ref, f32[2,256]{1,0:T(2,128)S(1)} %get-tuple-element.65.wt_ref, f32[1,4096]{1,0:T(1,128)S(1)} %bitcast.124, bf16[2,704,4096]{2,1,0:T(8,128)(2,1)} %bitcast.134, ...), custom_call_target="tpu_custom_call" | custom-call | flops 8858370048 | bytes 34603008 | tf_op jit(solution)/shard_map/expert/pallas_call | solution.py:256
  237.5 15.8 %expert.7 = (bf16[4,2,32,2048]{3,2,1,0:T(8,128)(2,1)S(1)}, bf16[4,2,32,2048]{3,2,1,0:T(8,128)(2,1)S(1)}) custom-call(s32[8]{0:T(128)S(1)} %concatenate.35.order_ref, f32[2,256]{1,0:T(2,128)S(1)} %get-tuple-element.66.wt_ref, f32[1,4096]{1,0:T(1,128)S(1)} %bitcast.125, bf16[2,704,4096]{2,1,0:T(8,128)(2,1)} %bitcast.135, bf16[2,704,4096]{2,1,0:T(8,128)(2,1)} %bitcast.139, ...), custom_call_target="tpu_custom_call" | custom-call | flops 8858370048 | bytes 34603008 | tf_op jit(solution)/shard_map/expert/pallas_call | solution.py:256
  253.3 15.8 %expert.6 = (bf16[4,2,32,2048]{3,2,1,0:T(8,128)(2,1)S(1)}, bf16[4,2,32,2048]{3,2,1,0:T(8,128)(2,1)S(1)}) custom-call(s32[8]{0:T(128)S(1)} %concatenate.35.order_ref, f32[2,256]{1,0:T(2,128)S(1)} %get-tuple-element.64.wt_ref, f32[1,4096]{1,0:T(1,128)S(1)} %bitcast.126, bf16[2,704,4096]{2,1,0:T(8,128)(2,1)} %bitcast.136, bf16[2,704,4096]{2,1,0:T(8,128)(2,1)} %bitcast.140, ...), custom_call_target="tpu_custom_call" | custom-call | flops 8858370048 | bytes 34603008 | tf_op jit(solution)/shard_map/expert/pallas_call | solution.py:256
  269.7 16.7 %expert.5 = (bf16[4,2,32,2048]{3,2,1,0:T(8,128)(2,1)S(1)}, bf16[4,2,32,2048]{3,2,1,0:T(8,128)(2,1)}, bf16[2,32,2048]{2,1,0:T(8,128)(2,1)S(1)}) custom-call(s32[8]{0:T(128)S(1)} %concatenate.35.order_ref, f32[2,256]{1,0:T(2,128)S(1)} %get-tuple-element.67.wt_ref, f32[1,4096]{1,0:T(1,128)S(1)} %bitcast.127, bf16[2,704,4096]{2,1,0:T(8,128)(2,1)} %bitcast.137, ...), custom_call_target="tpu_custom_call" | custom-call | flops 8858370048 | bytes 34603008 | tf_op jit(solution)/shard_map/expert/pallas_call | solution.py:256
  289.4 23.5 %collective-permute-done.44.refs_0_ = bf16[4,2,32,2048]{3,2,1,0:T(8,128)(2,1)S(1)} collective-permute-done((bf16[4,2,32,2048]{3,2,1,0:T(8,128)(2,1)S(1)}, bf16[4,2,32,2048]{3,2,1,0:T(8,128)(2,1)S(1)}, u32[]{:S(2)}, u32[]{:S(2)}) %collective-permute-start.44) | collective-permute-done | bytes 1048608 | tf_op jit(solution)/shard_map/ppermute | solution.py:339
  314.3 6.2 %collective-permute-start.45 = (bf16[2,32,2048]{2,1,0:T(8,128)(2,1)S(1)}, bf16[2,32,2048]{2,1,0:T(8,128)(2,1)S(1)}, u32[]{:S(2)}, u32[]{:S(2)}) collective-permute-start(bf16[2,32,2048]{2,1,0:T(8,128)(2,1)S(1)} %get-tuple-element.46), channel_id=1, source_target_pairs={{0,4},{2,6},{4,8},{6,10},{8,12},{10,14},{12,0},{14,2},{1,5},{3,7},... | collective-permute-start | bytes 786440 | tf_op jit(solution)/shard_map/ppermute | solution.py:336
  321.3 13.6 %collective-permute-done.34.refs_0_ = bf16[4,2,32,2048]{3,2,1,0:T(8,128)(2,1)S(1)} collective-permute-done((bf16[4,2,32,2048]{3,2,1,0:T(8,128)(2,1)S(1)}, bf16[4,2,32,2048]{3,2,1,0:T(8,128)(2,1)S(1)}, u32[]{:S(2)}, u32[]{:S(2)}) %collective-permute-start.34) | collective-permute-done | bytes 1048608 | tf_op jit(solution)/shard_map/ppermute | solution.py:339
  336.2 6.2 %collective-permute-start.35 = (bf16[2,32,2048]{2,1,0:T(8,128)(2,1)S(1)}, bf16[2,32,2048]{2,1,0:T(8,128)(2,1)S(1)}, u32[]{:S(2)}, u32[]{:S(2)}) collective-permute-start(bf16[2,32,2048]{2,1,0:T(8,128)(2,1)S(1)} %get-tuple-element.37), channel_id=1, source_target_pairs={{0,4},{2,6},{4,8},{6,10},{8,12},{10,14},{12,0},{14,2},{1,5},{3,7},... | collective-permute-start | bytes 786440 | tf_op jit(solution)/shard_map/ppermute | solution.py:336
  350.1 10.2 %collective-permute-done.36 = bf16[2,32,2048]{2,1,0:T(8,128)(2,1)S(1)} collective-permute-done((bf16[2,32,2048]{2,1,0:T(8,128)(2,1)S(1)}, bf16[2,32,2048]{2,1,0:T(8,128)(2,1)S(1)}, u32[]{:S(2)}, u32[]{:S(2)}) %collective-permute-start.36) | collective-permute-done | bytes 262176 | tf_op jit(solution)/shard_map/ppermute | solution.py:336
  360.6 6.1 %collective-permute-done.47 = bf16[2,32,2048]{2,1,0:T(8,128)(2,1)S(1)} collective-permute-done((bf16[2,32,2048]{2,1,0:T(8,128)(2,1)S(1)}, bf16[2,32,2048]{2,1,0:T(8,128)(2,1)S(1)}, u32[]{:S(2)}, u32[]{:S(2)}) %collective-permute-start.47) | collective-permute-done | bytes 262176 | tf_op jit(solution)/shard_map/ppermute | solution.py:336
  366.8 4.8 %collective-permute-done.46 = bf16[2,32,2048]{2,1,0:T(8,128)(2,1)S(1)} collective-permute-done((bf16[2,32,2048]{2,1,0:T(8,128)(2,1)S(1)}, bf16[2,32,2048]{2,1,0:T(8,128)(2,1)S(1)}, u32[]{:S(2)}, u32[]{:S(2)}) %collective-permute-start.46) | collective-permute-done | bytes 262176 | tf_op jit(solution)/shard_map/ppermute | solution.py:336
  (194 shorter events, 112.7 us)
Async XLA Ops:
  3.1 91.8 %collective-permute-start.4 = (bf16[2,32,1024]{2,1,0:T(8,128)(2,1)}, bf16[2,32,1024]{2,1,0:T(8,128)(2,1)}, u32[]{:S(2)}, u32[]{:S(2)}) collective-permute-start(bf16[2,32,1024]{2,1,0:T(8,128)(2,1)} %get-tuple-element.50), channel_id=1, source_target_pairs={{0,4},{2,6},{4,8},{6,10},{8,12},{10,14},{12,0},{14,2},{1,5},{3,7},... | collective-permute-start | bytes 393224 | tf_op jit(solution)/shard_map/ppermute | solution.py:336
  8.0 102.5 %collective-permute-start.11 = (bf16[512,512]{1,0:T(8,128)(2,1)}, bf16[512,512]{1,0:T(8,128)(2,1)}, u32[]{:S(2)}, u32[]{:S(2)}) collective-permute-start(bf16[512,512]{1,0:T(8,128)(2,1)} %constant_dynamic-slice_fusion.3), channel_id=1, source_target_pairs={{0,2},{2,0},{4,6},{6,4},{8,10},{10,8},{12,14},{14,12},{1,3},{3,1},... | collective-permute-start | bytes 1572872 | tf_op jit(solution)/shard_map/ppermute | solution.py:339
  25.5 85.0 %collective-permute-start.7 = (bf16[64,3072]{1,0:T(8,128)(2,1)S(1)}, bf16[64,3072]{1,0:T(8,128)(2,1)}, u32[]{:S(2)}, u32[]{:S(2)}) collective-permute-start(bf16[64,3072]{1,0:T(8,128)(2,1)S(1)} %attend.2.refs_0_), channel_id=1, source_target_pairs={{0,4},{2,6},{4,8},{6,10},{8,12},{10,14},{12,0},{14,2},{1,5},{3,7},... | collective-permute-start | bytes 1179656 | tf_op jit(solution)/shard_map/ppermute | solution.py:336
  28.6 102.8 %collective-permute-start.10 = (bf16[2048,512]{1,0:T(8,128)(2,1)}, bf16[2048,512]{1,0:T(8,128)(2,1)}, u32[]{:S(2)}, u32[]{:S(2)}) collective-permute-start(bf16[2048,512]{1,0:T(8,128)(2,1)} %slice.66), channel_id=1, source_target_pairs={{0,2},{2,0},{4,6},{6,4},{8,10},{10,8},{12,14},{14,12},{1,3},{3,1},... | collective-permute-start | bytes 6291464 | tf_op jit(solution)/shard_map/ppermute | solution.py:339
  29.7 45.9 %collective-permute-start = (f32[128,16]{0,1:T(8,128)}, f32[128,16]{0,1:T(8,128)}, u32[]{:S(2)}, u32[]{:S(2)}) collective-permute-start(f32[128,16]{0,1:T(8,128)} %get-tuple-element.69), channel_id=1, source_target_pairs={{0,2},{2,0},{4,6},{6,4},{8,10},{10,8},{12,14},{14,12},{1,3},{3,1},... | collective-permute-start | bytes 24584 | tf_op jit(solution)/shard_map/ppermute | solution.py:339
  110.5 20.9 %collective-permute-start.8 = (bf16[64,3072]{1,0:T(8,128)(2,1)}, bf16[64,3072]{1,0:T(8,128)(2,1)S(1)}, u32[]{:S(2)}, u32[]{:S(2)}) collective-permute-start(bf16[64,3072]{1,0:T(8,128)(2,1)} %collective-permute-done.7.refs_1_), channel_id=1, source_target_pairs={{0,4},{2,6},{4,8},{6,10},{8,12},{10,14},{12,0},{14,2},{1,5},{3,7},... | collective-permute-start | bytes 1179656 | tf_op jit(solution)/shard_map/ppermute | solution.py:336
  110.5 20.9 %collective-permute-start.12 = (bf16[512,512]{1,0:T(8,128)(2,1)}, bf16[512,512]{1,0:T(8,128)(2,1)S(1)}, u32[]{:S(2)}, u32[]{:S(2)}) collective-permute-start(bf16[512,512]{1,0:T(8,128)(2,1)} %collective-permute-done.11.refs_5_), channel_id=1, source_target_pairs={{0,16},{16,0},{1,17},{17,1},{2,18},{18,2},{3,19},{19,3},{4,20},{20... | collective-permute-start | bytes 1572872 | tf_op jit(solution)/shard_map/ppermute | solution.py:343
  153.4 35.9 %collective-permute-start.24 = (bf16[4,32,1024]{2,1,0:T(8,128)(2,1)S(1)}, bf16[4,32,1024]{2,1,0:T(8,128)(2,1)S(1)}, u32[]{:S(2)}, u32[]{:S(2)}) collective-permute-start(bf16[4,32,1024]{2,1,0:T(8,128)(2,1)S(1)} %fusion.refs_0_), channel_id=1, source_target_pairs={{0,8},{2,10},{4,12},{6,14},{8,0},{10,2},{12,4},{14,6},{1,9},{3,11}... | collective-permute-start | bytes 786440 | tf_op jit(solution)/shard_map/ppermute | solution.py:336
  156.2 33.1 %collective-permute-start.25 = (bf16[4,32,1024]{2,1,0:T(8,128)(2,1)S(1)}, bf16[4,32,1024]{2,1,0:T(8,128)(2,1)S(1)}, u32[]{:S(2)}, u32[]{:S(2)}) collective-permute-start(bf16[4,32,1024]{2,1,0:T(8,128)(2,1)S(1)} %fusion.refs_0_), channel_id=1, source_target_pairs={{0,12},{2,14},{4,0},{6,2},{8,4},{10,6},{12,8},{14,10},{1,13},{3,15... | collective-permute-start | bytes 786440 | tf_op jit(solution)/shard_map/ppermute | solution.py:336
  167.5 48.5 %collective-permute-start.18 = (bf16[3,4,32,1024]{3,2,1,0:T(8,128)(2,1)S(1)}, bf16[3,4,32,1024]{3,2,1,0:T(8,128)(2,1)}, u32[]{:S(2)}, u32[]{:S(2)}) collective-permute-start(bf16[3,4,32,1024]{3,2,1,0:T(8,128)(2,1)S(1)} %pad_maximum_fusion.refs_1_), channel_id=1, source_target_pairs={{0,1},{1,0},{2,3},{3,2},{4,5},{5,4},{6,7},{7,6},{8,9},{9,8},{10,11... | collective-permute-start | bytes 2359304 | tf_op jit(solution)/shard_map/ppermute | solution.py:341
  189.4 26.6 %collective-permute-start.40 = (bf16[3,4,32,1024]{3,2,1,0:T(8,128)(2,1)S(1)}, bf16[3,4,32,1024]{3,2,1,0:T(8,128)(2,1)S(1)}, u32[]{:S(2)}, u32[]{:S(2)}) collective-permute-start(bf16[3,4,32,1024]{3,2,1,0:T(8,128)(2,1)S(1)} %pad_maximum_fusion.1.refs_1_), channel_id=1, source_target_pairs={{0,2},{2,0},{4,6},{6,4},{8,10},{10,8},{12,14},{14,12},{1,3},{3,1},... | collective-permute-start | bytes 2359304 | tf_op jit(solution)/shard_map/ppermute | solution.py:339
  190.4 25.1 %collective-permute-start.39 = (bf16[4,32,1024]{2,1,0:T(8,128)(2,1)S(1)}, bf16[4,32,1024]{2,1,0:T(8,128)(2,1)S(1)}, u32[]{:S(2)}, u32[]{:S(2)}) collective-permute-start(bf16[4,32,1024]{2,1,0:T(8,128)(2,1)S(1)} %fusion.refs_0_), channel_id=1, source_target_pairs={{0,2},{2,0},{4,6},{6,4},{8,10},{10,8},{12,14},{14,12},{1,3},{3,1},... | collective-permute-start | bytes 786440 | tf_op jit(solution)/shard_map/ppermute | solution.py:339
  192.1 41.6 %collective-permute-start.29 = (bf16[4,32,1024]{2,1,0:T(8,128)(2,1)S(1)}, bf16[4,32,1024]{2,1,0:T(8,128)(2,1)S(1)}, u32[]{:S(2)}, u32[]{:S(2)}) collective-permute-start(bf16[4,32,1024]{2,1,0:T(8,128)(2,1)S(1)} %fusion.1.refs_0_), channel_id=1, source_target_pairs={{0,2},{2,0},{4,6},{6,4},{8,10},{10,8},{12,14},{14,12},{1,3},{3,1},... | collective-permute-start | bytes 786440 | tf_op jit(solution)/shard_map/ppermute | solution.py:339
  192.7 77.0 %collective-permute-start.26 = (bf16[4,32,1024]{2,1,0:T(8,128)(2,1)S(1)}, bf16[4,32,1024]{2,1,0:T(8,128)(2,1)S(1)}, u32[]{:S(2)}, u32[]{:S(2)}) collective-permute-start(bf16[4,32,1024]{2,1,0:T(8,128)(2,1)S(1)} %fusion.refs_0_), channel_id=1, source_target_pairs={{0,1},{1,0},{2,3},{3,2},{4,5},{5,4},{6,7},{7,6},{8,9},{9,8},{10,11... | collective-permute-start | bytes 786440 | tf_op jit(solution)/shard_map/ppermute | solution.py:341
  215.5 21.5 %collective-permute-start.30 = (bf16[3,4,32,1024]{3,2,1,0:T(8,128)(2,1)S(1)}, bf16[3,4,32,1024]{3,2,1,0:T(8,128)(2,1)S(1)}, u32[]{:S(2)}, u32[]{:S(2)}) collective-permute-start(bf16[3,4,32,1024]{3,2,1,0:T(8,128)(2,1)S(1)} %pad_maximum_fusion.refs_1_), channel_id=1, source_target_pairs={{0,2},{2,0},{4,6},{6,4},{8,10},{10,8},{12,14},{14,12},{1,3},{3,1},... | collective-permute-start | bytes 2359304 | tf_op jit(solution)/shard_map/ppermute | solution.py:339
  216.0 21.0 %collective-permute-start.42 = (bf16[3,4,32,1024]{3,2,1,0:T(8,128)(2,1)S(1)}, bf16[3,4,32,1024]{3,2,1,0:T(8,128)(2,1)S(1)}, u32[]{:S(2)}, u32[]{:S(2)}) collective-permute-start(bf16[3,4,32,1024]{3,2,1,0:T(8,128)(2,1)S(1)} %collective-permute-done.40.refs_1_), channel_id=1, source_target_pairs={{0,1},{1,0},{2,3},{3,2},{4,5},{5,4},{6,7},{7,6},{8,9},{9,8},{10,11... | collective-permute-start | bytes 2359304 | tf_op jit(solution)/shard_map/ppermute | solution.py:341
  233.7 36.0 %collective-permute-start.27 = (bf16[3,4,32,1024]{3,2,1,0:T(8,128)(2,1)S(1)}, bf16[3,4,32,1024]{3,2,1,0:T(8,128)(2,1)S(1)}, u32[]{:S(2)}, u32[]{:S(2)}) collective-permute-start(bf16[3,4,32,1024]{3,2,1,0:T(8,128)(2,1)S(1)} %pad_maximum_fusion.1.refs_1_), channel_id=1, source_target_pairs={{0,1},{1,0},{2,3},{3,2},{4,5},{5,4},{6,7},{7,6},{8,9},{9,8},{10,11... | collective-permute-start | bytes 2359304 | tf_op jit(solution)/shard_map/ppermute | solution.py:341
  237.0 84.4 %collective-permute-start.28 = (bf16[4,2,32,2048]{3,2,1,0:T(8,128)(2,1)S(1)}, bf16[4,2,32,2048]{3,2,1,0:T(8,128)(2,1)S(1)}, u32[]{:S(2)}, u32[]{:S(2)}) collective-permute-start(bf16[4,2,32,2048]{3,2,1,0:T(8,128)(2,1)S(1)} %get-tuple-element.33), channel_id=1, source_target_pairs={{0,1},{1,0},{2,3},{3,2},{4,5},{5,4},{6,7},{7,6},{8,9},{9,8},{10,11... | collective-permute-start | bytes 3145736 | tf_op jit(solution)/shard_map/ppermute | solution.py:341
  253.2 33.2 %collective-permute-start.43 = (bf16[4,2,32,2048]{3,2,1,0:T(8,128)(2,1)S(1)}, bf16[4,2,32,2048]{3,2,1,0:T(8,128)(2,1)S(1)}, u32[]{:S(2)}, u32[]{:S(2)}) collective-permute-start(bf16[4,2,32,2048]{3,2,1,0:T(8,128)(2,1)S(1)} %get-tuple-element.43), channel_id=1, source_target_pairs={{0,1},{1,0},{2,3},{3,2},{4,5},{5,4},{6,7},{7,6},{8,9},{9,8},{10,11... | collective-permute-start | bytes 3145736 | tf_op jit(solution)/shard_map/ppermute | solution.py:341
  286.9 26.1 %collective-permute-start.44 = (bf16[4,2,32,2048]{3,2,1,0:T(8,128)(2,1)S(1)}, bf16[4,2,32,2048]{3,2,1,0:T(8,128)(2,1)S(1)}, u32[]{:S(2)}, u32[]{:S(2)}) collective-permute-start(bf16[4,2,32,2048]{3,2,1,0:T(8,128)(2,1)S(1)} %add_convert_fusion), channel_id=1, source_target_pairs={{0,2},{2,0},{4,6},{6,4},{8,10},{10,8},{12,14},{14,12},{1,3},{3,1},... | collective-permute-start | bytes 3145736 | tf_op jit(solution)/shard_map/ppermute | solution.py:339
  287.9 47.1 %collective-permute-start.34 = (bf16[4,2,32,2048]{3,2,1,0:T(8,128)(2,1)S(1)}, bf16[4,2,32,2048]{3,2,1,0:T(8,128)(2,1)S(1)}, u32[]{:S(2)}, u32[]{:S(2)}) collective-permute-start(bf16[4,2,32,2048]{3,2,1,0:T(8,128)(2,1)S(1)} %add_convert_fusion.1), channel_id=1, source_target_pairs={{0,2},{2,0},{4,6},{6,4},{8,10},{10,8},{12,14},{14,12},{1,3},{3,1},... | collective-permute-start | bytes 3145736 | tf_op jit(solution)/shard_map/ppermute | solution.py:339
  314.3 32.6 %collective-permute-start.45 = (bf16[2,32,2048]{2,1,0:T(8,128)(2,1)S(1)}, bf16[2,32,2048]{2,1,0:T(8,128)(2,1)S(1)}, u32[]{:S(2)}, u32[]{:S(2)}) collective-permute-start(bf16[2,32,2048]{2,1,0:T(8,128)(2,1)S(1)} %get-tuple-element.46), channel_id=1, source_target_pairs={{0,4},{2,6},{4,8},{6,10},{8,12},{10,14},{12,0},{14,2},{1,5},{3,7},... | collective-permute-start | bytes 786440 | tf_op jit(solution)/shard_map/ppermute | solution.py:336
  344.9 21.9 %collective-permute-start.47 = (bf16[2,32,2048]{2,1,0:T(8,128)(2,1)S(1)}, bf16[2,32,2048]{2,1,0:T(8,128)(2,1)S(1)}, u32[]{:S(2)}, u32[]{:S(2)}) collective-permute-start(bf16[2,32,2048]{2,1,0:T(8,128)(2,1)S(1)} %get-tuple-element.47), channel_id=1, source_target_pairs={{0,12},{2,14},{4,0},{6,2},{8,4},{10,6},{12,8},{14,10},{1,13},{3,15... | collective-permute-start | bytes 786440 | tf_op jit(solution)/shard_map/ppermute | solution.py:336
  346.9 24.7 %collective-permute-start.46 = (bf16[2,32,2048]{2,1,0:T(8,128)(2,1)S(1)}, bf16[2,32,2048]{2,1,0:T(8,128)(2,1)S(1)}, u32[]{:S(2)}, u32[]{:S(2)}) collective-permute-start(bf16[2,32,2048]{2,1,0:T(8,128)(2,1)S(1)} %add_convert_fusion.3), channel_id=1, source_target_pairs={{0,4},{2,6},{4,8},{6,10},{8,12},{10,14},{12,0},{14,2},{1,5},{3,7},... | collective-permute-start | bytes 786440 | tf_op jit(solution)/shard_map/ppermute | solution.py:336
  (51 other events, 609.1 us)

commit v2 on v1

--- a/solution.py
+++ b/solution.py
@@ -74,7 +74,7 @@
         grid_spec=pltpu.PrefetchScalarGridSpec(num_scalar_prefetch=1, grid=(1,),
             in_specs=[whole(q), kspec, kspec, whole(fk), whole(fv)], out_specs=whole(q),
             scratch_shapes=[pltpu.VMEM((kv, rows // kv, hd), jnp.bfloat16)] * 2),
-        compiler_params=pltpu.CompilerParams(vmem_limit_bytes=VMEM // 2),
+        compiler_params=pltpu.CompilerParams(vmem_limit_bytes=VMEM * 2 // 5),
         cost_estimate=cost(4 * tok * wide * (rows // kv), 4 * rows * hd, tok * wide // hd * (rows // kv)), name="attend")(lengths, q, keys, values, fk, fv)
 
 
@@ -273,7 +273,7 @@
             pltpu.SemaphoreType.DMA((2, 2)),
             pltpu.SemaphoreType.DMA((2,)),
         ],
-        compiler_params=pltpu.CompilerParams(vmem_limit_bytes=min(VMEM, held + (8 << 20))),
+        compiler_params=pltpu.CompilerParams(vmem_limit_bytes=min(VMEM, held + (5 << 20))),
         cost_estimate=cost(6 * rows * depth * ff * experts, 6 * depth * ff * experts),
         name="expert",
     )(order, wt, gain, gate_t, up_t, down_w, *p)
@@ -312,7 +312,7 @@
         grid_spec=pltpu.PrefetchScalarGridSpec(
             num_scalar_prefetch=1, grid=(steps,), in_specs=[block] * (2 + len(extra)), out_specs=specs
         ),
-        compiler_params=pltpu.CompilerParams(vmem_limit_bytes=VMEM // 2),
+        compiler_params=pltpu.CompilerParams(vmem_limit_bytes=min(VMEM // 2, 16 * ours.size + (4 << 20))),
         cost_estimate=cost(4 * ours.size, 2 * ours.size * (3 + len(extra))),
         name="settle",
     )(order, ours, theirs, *extra)

time: 377 us -> 376 us (level)
    unnamed x60 -> x56, local copies, waits for them, and re-layouts: 14.9 us -> 14.8 us
where the time goes in v2:
time: 376 us; the launch traced here: 372 us
  waiting for transfers between devices  169 us (45%)
  Pallas kernels  95.1 us (25%)
  starting transfers between devices  64.8 us (17%)
  local copies, waits for them, and re-layouts  30.8 us (8%)
  other arithmetic  11 us (3%)
    ppermute x24, waiting for transfers between devices, shift(): return lax.ppermute(x, 'dev', pairs)  84.5 us
    ppermute x9, waiting for transfers between devices, across(): lax.ppermute(x, 'dev', [(a * ny + b, a * ny + (b + 1) % ny) for a in rang...  84.2 us
    pallas_call x4, Pallas kernels, expert(): pl.pallas_call(functools.partial(expert_body, nz=nz, eps=1e-05, show=show...  63.4 us
    ppermute x24, starting transfers between devices, shift(): return lax.ppermute(x, 'dev', pairs)  51.9 us
    pallas_call x2, Pallas kernels, attend(): pl.pallas_call(functools.partial(attend_body, seq=seq, kv=kv, heads=heads...  21 us
    unnamed x56, local copies, waits for them, and re-layouts  14.8 us
    ppermute x9, starting transfers between devices, across(): lax.ppermute(x, 'dev', [(a * ny + b, a * ny + (b + 1) % ny) for a in rang...  8.86 us
    pallas_call x2, Pallas kernels, project(): pl.pallas_call(functools.partial(project_body, nz=nz), out_shape=(jax.Sha...  8.14 us
  transfers between devices with their start and end apart: 48, of which 22 were waited for; matrix products, arithmetic and copies ran while one was open for 8% of the time, Pallas kernels for 26%

profile of v2, /device:TPU:0, one launch (start us, length us, event | category | flops | bytes accessed | tf_op | source)
XLA Modules:
  0.0 371.6 jit_solution(174238026707223712)
XLA Ops:
  14.9 10.5 %attend.2.refs_0_ = bf16[64,3072]{1,0:T(8,128)(2,1)S(1)} custom-call(s32[2]{0:T(128)S(1)} %copy-done.12, bf16[64,3072]{1,0:T(8,128)(2,1)S(1)} %bitcast.123, bf16[2,4096,128]{2,1,0:T(8,128)(2,1)S(1)} %bitcast.130, bf16[2,4096,128]{2,1,0:T(8,128)(2,1)S(1)} %bitcast.132, bf16[64,256]{1,0:T(8,128)(2,1)S(1)} %get-tuple-element.73.nk_ref, ...), custom_call_target="tpu_custom_call" | custom-call | flops 1610612736 | bytes 2097152 | tf_op jit(solution)/shard_map/attend/pallas_call | solution.py:71
  42.0 10.5 %attend.3.refs_0_ = bf16[64,3072]{1,0:T(8,128)(2,1)S(1)} custom-call(s32[2]{0:T(128)S(1)} %copy-done.12, bf16[64,3072]{1,0:T(8,128)(2,1)S(1)} %bitcast.122, bf16[2,4096,128]{2,1,0:T(8,128)(2,1)S(1)} %bitcast.131, bf16[2,4096,128]{2,1,0:T(8,128)(2,1)S(1)} %bitcast.133, bf16[64,256]{1,0:T(8,128)(2,1)S(1)} %copy-done.7, bf16[64,256]{1,0:T(8,128)(2,1)S(1)} %copy-done.6), custom_call_target="tpu_custom_call" | custom-call | flops 1610612736 | bytes 2097152 | tf_op jit(solution)/shard_map/attend/pallas_call | solution.py:71
  55.2 20.4 %collective-permute-done = f32[128,16]{0,1:T(8,128)} collective-permute-done((f32[128,16]{0,1:T(8,128)}, f32[128,16]{0,1:T(8,128)}, u32[]{:S(2)}, u32[]{:S(2)}) %collective-permute-start) | collective-permute-done | bytes 8224 | tf_op jit(solution)/shard_map/ppermute | solution.py:339
  82.5 4.0 %collective-permute-done.2 = f32[2,128,16]{1,2,0:T(8,128)S(1)} collective-permute-done((f32[2,128,16]{1,2,0:T(8,128)S(1)}, f32[2,128,16]{1,2,0:T(8,128)S(1)}, u32[]{:S(2)}, u32[]{:S(2)}) %collective-permute-start.2) | collective-permute-done | bytes 16416 | tf_op jit(solution)/shard_map/ppermute | solution.py:336
  99.7 7.2 %collective-permute-start.9 = (bf16[64,3072]{1,0:T(8,128)(2,1)S(1)}, bf16[64,3072]{1,0:T(8,128)(2,1)S(1)}, u32[]{:S(2)}, u32[]{:S(2)}) collective-permute-start(bf16[64,3072]{1,0:T(8,128)(2,1)S(1)} %attend.2.refs_0_), channel_id=1, source_target_pairs={{0,12},{2,14},{4,0},{6,2},{8,4},{10,6},{12,8},{14,10},{1,13},{3,15... | collective-permute-start | bytes 1179656 | tf_op jit(solution)/shard_map/ppermute | solution.py:336
  116.5 4.3 %collective-permute-start.21 = (bf16[64,3072]{1,0:T(8,128)(2,1)}, bf16[64,3072]{1,0:T(8,128)(2,1)S(1)}, u32[]{:S(2)}, u32[]{:S(2)}) collective-permute-start(bf16[64,3072]{1,0:T(8,128)(2,1)} %copy-done.2), channel_id=1, source_target_pairs={{0,12},{2,14},{4,0},{6,2},{8,4},{10,6},{12,8},{14,10},{1,13},{3,15... | collective-permute-start | bytes 1179656 | tf_op jit(solution)/shard_map/ppermute | solution.py:336
  120.8 4.2 %collective-permute-done.19.refs_1_ = bf16[64,3072]{1,0:T(8,128)(2,1)S(1)} collective-permute-done((bf16[64,3072]{1,0:T(8,128)(2,1)}, bf16[64,3072]{1,0:T(8,128)(2,1)S(1)}, u32[]{:S(2)}, u32[]{:S(2)}) %collective-permute-start.19) | collective-permute-done | bytes 393248 | tf_op jit(solution)/shard_map/ppermute | solution.py:336
  131.4 4.1 %project.2 = (f32[4,32,1024]{2,1,0:T(8,128)S(1)}, bf16[4,32,1024]{2,1,0:T(8,128)(2,1)S(1)}) custom-call(s32[8]{0:T(128)S(1)} %concatenate.35.order_ref, bf16[3072,512]{1,0:T(8,128)(2,1)S(1)} %copy-done, bf16[64,3072]{1,0:T(8,128)(2,1)S(1)} %attend.2.refs_0_, bf16[64,3072]{1,0:T(8,128)(2,1)} %collective-permute-done.7.refs_1_, ...), custom_call_target="tpu_custom_call" | custom-call | flops 1610612736 | bytes 7864320 | tf_op jit(solution)/shard_map/project/pallas_call | solution.py:116
  135.7 4.2 %collective-permute-done.20.refs_2_ = bf16[64,3072]{1,0:T(8,128)(2,1)S(1)} collective-permute-done((bf16[64,3072]{1,0:T(8,128)(2,1)S(1)}, bf16[64,3072]{1,0:T(8,128)(2,1)S(1)}, u32[]{:S(2)}, u32[]{:S(2)}) %collective-permute-start.20) | collective-permute-done | bytes 393248 | tf_op jit(solution)/shard_map/ppermute | solution.py:336
  158.9 8.5 %collective-permute-done.15 = bf16[4,32,1024]{2,1,0:T(8,128)(2,1)S(1)} collective-permute-done((bf16[4,32,1024]{2,1,0:T(8,128)(2,1)S(1)}, bf16[4,32,1024]{2,1,0:T(8,128)(2,1)S(1)}, u32[]{:S(2)}, u32[]{:S(2)}) %collective-permute-start.15) | collective-permute-done | bytes 262176 | tf_op jit(solution)/shard_map/ppermute | solution.py:336
  167.6 5.5 %collective-permute-done.23 = bf16[4,32,1024]{2,1,0:T(8,128)(2,1)S(1)} collective-permute-done((bf16[4,32,1024]{2,1,0:T(8,128)(2,1)S(1)}, bf16[4,32,1024]{2,1,0:T(8,128)(2,1)S(1)}, u32[]{:S(2)}, u32[]{:S(2)}) %collective-permute-start.23) | collective-permute-done | bytes 262176 | tf_op jit(solution)/shard_map/ppermute | solution.py:336
  173.1 16.2 %collective-permute-done.24 = bf16[4,32,1024]{2,1,0:T(8,128)(2,1)S(1)} collective-permute-done((bf16[4,32,1024]{2,1,0:T(8,128)(2,1)S(1)}, bf16[4,32,1024]{2,1,0:T(8,128)(2,1)S(1)}, u32[]{:S(2)}, u32[]{:S(2)}) %collective-permute-start.24) | collective-permute-done | bytes 262176 | tf_op jit(solution)/shard_map/ppermute | solution.py:336
  192.6 22.8 %collective-permute-done.39.refs_0_ = bf16[4,32,1024]{2,1,0:T(8,128)(2,1)S(1)} collective-permute-done((bf16[4,32,1024]{2,1,0:T(8,128)(2,1)S(1)}, bf16[4,32,1024]{2,1,0:T(8,128)(2,1)S(1)}, u32[]{:S(2)}, u32[]{:S(2)}) %collective-permute-start.39) | collective-permute-done | bytes 262176 | tf_op jit(solution)/shard_map/ppermute | solution.py:339
  216.5 16.1 %expert.4 = (bf16[4,2,32,2048]{3,2,1,0:T(8,128)(2,1)S(1)}, bf16[4,2,32,2048]{3,2,1,0:T(8,128)(2,1)S(1)}, bf16[2,32,2048]{2,1,0:T(8,128)(2,1)S(1)}) custom-call(s32[8]{0:T(128)S(1)} %concatenate.35.order_ref, f32[2,256]{1,0:T(2,128)S(1)} %get-tuple-element.65.wt_ref, f32[1,4096]{1,0:T(1,128)S(1)} %bitcast.124, bf16[2,704,4096]{2,1,0:T(8,128)(2,1)} %bitcast.134, ...), custom_call_target="tpu_custom_call" | custom-call | flops 8858370048 | bytes 34603008 | tf_op jit(solution)/shard_map/expert/pallas_call | solution.py:256
  237.5 15.7 %expert.7 = (bf16[4,2,32,2048]{3,2,1,0:T(8,128)(2,1)S(1)}, bf16[4,2,32,2048]{3,2,1,0:T(8,128)(2,1)S(1)}) custom-call(s32[8]{0:T(128)S(1)} %concatenate.35.order_ref, f32[2,256]{1,0:T(2,128)S(1)} %get-tuple-element.66.wt_ref, f32[1,4096]{1,0:T(1,128)S(1)} %bitcast.125, bf16[2,704,4096]{2,1,0:T(8,128)(2,1)} %bitcast.135, bf16[2,704,4096]{2,1,0:T(8,128)(2,1)} %bitcast.139, ...), custom_call_target="tpu_custom_call" | custom-call | flops 8858370048 | bytes 34603008 | tf_op jit(solution)/shard_map/expert/pallas_call | solution.py:256
  253.3 15.8 %expert.6 = (bf16[4,2,32,2048]{3,2,1,0:T(8,128)(2,1)S(1)}, bf16[4,2,32,2048]{3,2,1,0:T(8,128)(2,1)S(1)}) custom-call(s32[8]{0:T(128)S(1)} %concatenate.35.order_ref, f32[2,256]{1,0:T(2,128)S(1)} %get-tuple-element.64.wt_ref, f32[1,4096]{1,0:T(1,128)S(1)} %bitcast.126, bf16[2,704,4096]{2,1,0:T(8,128)(2,1)} %bitcast.136, bf16[2,704,4096]{2,1,0:T(8,128)(2,1)} %bitcast.140, ...), custom_call_target="tpu_custom_call" | custom-call | flops 8858370048 | bytes 34603008 | tf_op jit(solution)/shard_map/expert/pallas_call | solution.py:256
  269.6 15.8 %expert.5 = (bf16[4,2,32,2048]{3,2,1,0:T(8,128)(2,1)S(1)}, bf16[4,2,32,2048]{3,2,1,0:T(8,128)(2,1)S(1)}, bf16[2,32,2048]{2,1,0:T(8,128)(2,1)S(1)}) custom-call(s32[8]{0:T(128)S(1)} %concatenate.35.order_ref, f32[2,256]{1,0:T(2,128)S(1)} %get-tuple-element.67.wt_ref, f32[1,4096]{1,0:T(1,128)S(1)} %bitcast.127, bf16[2,704,4096]{2,1,0:T(8,128)(2,1)} %bitcast.137, ...), custom_call_target="tpu_custom_call" | custom-call | flops 8858370048 | bytes 34603008 | tf_op jit(solution)/shard_map/expert/pallas_call | solution.py:256
  288.5 23.5 %collective-permute-done.44.refs_0_ = bf16[4,2,32,2048]{3,2,1,0:T(8,128)(2,1)S(1)} collective-permute-done((bf16[4,2,32,2048]{3,2,1,0:T(8,128)(2,1)S(1)}, bf16[4,2,32,2048]{3,2,1,0:T(8,128)(2,1)S(1)}, u32[]{:S(2)}, u32[]{:S(2)}) %collective-permute-start.44) | collective-permute-done | bytes 1048608 | tf_op jit(solution)/shard_map/ppermute | solution.py:339
  313.3 6.2 %collective-permute-start.45 = (bf16[2,32,2048]{2,1,0:T(8,128)(2,1)S(1)}, bf16[2,32,2048]{2,1,0:T(8,128)(2,1)S(1)}, u32[]{:S(2)}, u32[]{:S(2)}) collective-permute-start(bf16[2,32,2048]{2,1,0:T(8,128)(2,1)S(1)} %get-tuple-element.46), channel_id=1, source_target_pairs={{0,4},{2,6},{4,8},{6,10},{8,12},{10,14},{12,0},{14,2},{1,5},{3,7},... | collective-permute-start | bytes 786440 | tf_op jit(solution)/shard_map/ppermute | solution.py:336
  320.3 13.6 %collective-permute-done.34.refs_0_ = bf16[4,2,32,2048]{3,2,1,0:T(8,128)(2,1)S(1)} collective-permute-done((bf16[4,2,32,2048]{3,2,1,0:T(8,128)(2,1)S(1)}, bf16[4,2,32,2048]{3,2,1,0:T(8,128)(2,1)S(1)}, u32[]{:S(2)}, u32[]{:S(2)}) %collective-permute-start.34) | collective-permute-done | bytes 1048608 | tf_op jit(solution)/shard_map/ppermute | solution.py:339
  335.3 6.2 %collective-permute-start.35 = (bf16[2,32,2048]{2,1,0:T(8,128)(2,1)S(1)}, bf16[2,32,2048]{2,1,0:T(8,128)(2,1)S(1)}, u32[]{:S(2)}, u32[]{:S(2)}) collective-permute-start(bf16[2,32,2048]{2,1,0:T(8,128)(2,1)S(1)} %get-tuple-element.37), channel_id=1, source_target_pairs={{0,4},{2,6},{4,8},{6,10},{8,12},{10,14},{12,0},{14,2},{1,5},{3,7},... | collective-permute-start | bytes 786440 | tf_op jit(solution)/shard_map/ppermute | solution.py:336
  349.1 10.2 %collective-permute-done.36 = bf16[2,32,2048]{2,1,0:T(8,128)(2,1)S(1)} collective-permute-done((bf16[2,32,2048]{2,1,0:T(8,128)(2,1)S(1)}, bf16[2,32,2048]{2,1,0:T(8,128)(2,1)S(1)}, u32[]{:S(2)}, u32[]{:S(2)}) %collective-permute-start.36) | collective-permute-done | bytes 262176 | tf_op jit(solution)/shard_map/ppermute | solution.py:336
  359.7 6.1 %collective-permute-done.47 = bf16[2,32,2048]{2,1,0:T(8,128)(2,1)S(1)} collective-permute-done((bf16[2,32,2048]{2,1,0:T(8,128)(2,1)S(1)}, bf16[2,32,2048]{2,1,0:T(8,128)(2,1)S(1)}, u32[]{:S(2)}, u32[]{:S(2)}) %collective-permute-start.47) | collective-permute-done | bytes 262176 | tf_op jit(solution)/shard_map/ppermute | solution.py:336
  365.8 4.8 %collective-permute-done.46 = bf16[2,32,2048]{2,1,0:T(8,128)(2,1)S(1)} collective-permute-done((bf16[2,32,2048]{2,1,0:T(8,128)(2,1)S(1)}, bf16[2,32,2048]{2,1,0:T(8,128)(2,1)S(1)}, u32[]{:S(2)}, u32[]{:S(2)}) %collective-permute-start.46) | collective-permute-done | bytes 262176 | tf_op jit(solution)/shard_map/ppermute | solution.py:336
  (190 shorter events, 113.7 us)
Async XLA Ops:
  3.1 91.8 %collective-permute-start.4 = (bf16[2,32,1024]{2,1,0:T(8,128)(2,1)}, bf16[2,32,1024]{2,1,0:T(8,128)(2,1)}, u32[]{:S(2)}, u32[]{:S(2)}) collective-permute-start(bf16[2,32,1024]{2,1,0:T(8,128)(2,1)} %get-tuple-element.50), channel_id=1, source_target_pairs={{0,4},{2,6},{4,8},{6,10},{8,12},{10,14},{12,0},{14,2},{1,5},{3,7},... | collective-permute-start | bytes 393224 | tf_op jit(solution)/shard_map/ppermute | solution.py:336
  8.0 102.5 %collective-permute-start.11 = (bf16[512,512]{1,0:T(8,128)(2,1)}, bf16[512,512]{1,0:T(8,128)(2,1)}, u32[]{:S(2)}, u32[]{:S(2)}) collective-permute-start(bf16[512,512]{1,0:T(8,128)(2,1)} %constant_dynamic-slice_fusion.3), channel_id=1, source_target_pairs={{0,2},{2,0},{4,6},{6,4},{8,10},{10,8},{12,14},{14,12},{1,3},{3,1},... | collective-permute-start | bytes 1572872 | tf_op jit(solution)/shard_map/ppermute | solution.py:339
  25.5 85.0 %collective-permute-start.7 = (bf16[64,3072]{1,0:T(8,128)(2,1)S(1)}, bf16[64,3072]{1,0:T(8,128)(2,1)}, u32[]{:S(2)}, u32[]{:S(2)}) collective-permute-start(bf16[64,3072]{1,0:T(8,128)(2,1)S(1)} %attend.2.refs_0_), channel_id=1, source_target_pairs={{0,4},{2,6},{4,8},{6,10},{8,12},{10,14},{12,0},{14,2},{1,5},{3,7},... | collective-permute-start | bytes 1179656 | tf_op jit(solution)/shard_map/ppermute | solution.py:336
  28.6 102.9 %collective-permute-start.10 = (bf16[2048,512]{1,0:T(8,128)(2,1)}, bf16[2048,512]{1,0:T(8,128)(2,1)}, u32[]{:S(2)}, u32[]{:S(2)}) collective-permute-start(bf16[2048,512]{1,0:T(8,128)(2,1)} %slice.66), channel_id=1, source_target_pairs={{0,2},{2,0},{4,6},{6,4},{8,10},{10,8},{12,14},{14,12},{1,3},{3,1},... | collective-permute-start | bytes 6291464 | tf_op jit(solution)/shard_map/ppermute | solution.py:339
  29.7 45.9 %collective-permute-start = (f32[128,16]{0,1:T(8,128)}, f32[128,16]{0,1:T(8,128)}, u32[]{:S(2)}, u32[]{:S(2)}) collective-permute-start(f32[128,16]{0,1:T(8,128)} %get-tuple-element.69), channel_id=1, source_target_pairs={{0,2},{2,0},{4,6},{6,4},{8,10},{10,8},{12,14},{14,12},{1,3},{3,1},... | collective-permute-start | bytes 24584 | tf_op jit(solution)/shard_map/ppermute | solution.py:339
  110.4 21.0 %collective-permute-start.8 = (bf16[64,3072]{1,0:T(8,128)(2,1)}, bf16[64,3072]{1,0:T(8,128)(2,1)S(1)}, u32[]{:S(2)}, u32[]{:S(2)}) collective-permute-start(bf16[64,3072]{1,0:T(8,128)(2,1)} %collective-permute-done.7.refs_1_), channel_id=1, source_target_pairs={{0,4},{2,6},{4,8},{6,10},{8,12},{10,14},{12,0},{14,2},{1,5},{3,7},... | collective-permute-start | bytes 1179656 | tf_op jit(solution)/shard_map/ppermute | solution.py:336
  110.5 21.0 %collective-permute-start.12 = (bf16[512,512]{1,0:T(8,128)(2,1)}, bf16[512,512]{1,0:T(8,128)(2,1)S(1)}, u32[]{:S(2)}, u32[]{:S(2)}) collective-permute-start(bf16[512,512]{1,0:T(8,128)(2,1)} %collective-permute-done.11.refs_5_), channel_id=1, source_target_pairs={{0,16},{16,0},{1,17},{17,1},{2,18},{18,2},{3,19},{19,3},{4,20},{20... | collective-permute-start | bytes 1572872 | tf_op jit(solution)/shard_map/ppermute | solution.py:343
  153.4 35.9 %collective-permute-start.24 = (bf16[4,32,1024]{2,1,0:T(8,128)(2,1)S(1)}, bf16[4,32,1024]{2,1,0:T(8,128)(2,1)S(1)}, u32[]{:S(2)}, u32[]{:S(2)}) collective-permute-start(bf16[4,32,1024]{2,1,0:T(8,128)(2,1)S(1)} %fusion.refs_0_), channel_id=1, source_target_pairs={{0,8},{2,10},{4,12},{6,14},{8,0},{10,2},{12,4},{14,6},{1,9},{3,11}... | collective-permute-start | bytes 786440 | tf_op jit(solution)/shard_map/ppermute | solution.py:336
  156.2 33.1 %collective-permute-start.25 = (bf16[4,32,1024]{2,1,0:T(8,128)(2,1)S(1)}, bf16[4,32,1024]{2,1,0:T(8,128)(2,1)S(1)}, u32[]{:S(2)}, u32[]{:S(2)}) collective-permute-start(bf16[4,32,1024]{2,1,0:T(8,128)(2,1)S(1)} %fusion.refs_0_), channel_id=1, source_target_pairs={{0,12},{2,14},{4,0},{6,2},{8,4},{10,6},{12,8},{14,10},{1,13},{3,15... | collective-permute-start | bytes 786440 | tf_op jit(solution)/shard_map/ppermute | solution.py:336
  167.5 48.4 %collective-permute-start.18 = (bf16[3,4,32,1024]{3,2,1,0:T(8,128)(2,1)S(1)}, bf16[3,4,32,1024]{3,2,1,0:T(8,128)(2,1)}, u32[]{:S(2)}, u32[]{:S(2)}) collective-permute-start(bf16[3,4,32,1024]{3,2,1,0:T(8,128)(2,1)S(1)} %pad_maximum_fusion.refs_1_), channel_id=1, source_target_pairs={{0,1},{1,0},{2,3},{3,2},{4,5},{5,4},{6,7},{7,6},{8,9},{9,8},{10,11... | collective-permute-start | bytes 2359304 | tf_op jit(solution)/shard_map/ppermute | solution.py:341
  189.4 26.6 %collective-permute-start.40 = (bf16[3,4,32,1024]{3,2,1,0:T(8,128)(2,1)S(1)}, bf16[3,4,32,1024]{3,2,1,0:T(8,128)(2,1)S(1)}, u32[]{:S(2)}, u32[]{:S(2)}) collective-permute-start(bf16[3,4,32,1024]{3,2,1,0:T(8,128)(2,1)S(1)} %pad_maximum_fusion.1.refs_1_), channel_id=1, source_target_pairs={{0,2},{2,0},{4,6},{6,4},{8,10},{10,8},{12,14},{14,12},{1,3},{3,1},... | collective-permute-start | bytes 2359304 | tf_op jit(solution)/shard_map/ppermute | solution.py:339
  190.3 25.1 %collective-permute-start.39 = (bf16[4,32,1024]{2,1,0:T(8,128)(2,1)S(1)}, bf16[4,32,1024]{2,1,0:T(8,128)(2,1)S(1)}, u32[]{:S(2)}, u32[]{:S(2)}) collective-permute-start(bf16[4,32,1024]{2,1,0:T(8,128)(2,1)S(1)} %fusion.refs_0_), channel_id=1, source_target_pairs={{0,2},{2,0},{4,6},{6,4},{8,10},{10,8},{12,14},{14,12},{1,3},{3,1},... | collective-permute-start | bytes 786440 | tf_op jit(solution)/shard_map/ppermute | solution.py:339
  192.1 40.5 %collective-permute-start.29 = (bf16[4,32,1024]{2,1,0:T(8,128)(2,1)S(1)}, bf16[4,32,1024]{2,1,0:T(8,128)(2,1)S(1)}, u32[]{:S(2)}, u32[]{:S(2)}) collective-permute-start(bf16[4,32,1024]{2,1,0:T(8,128)(2,1)S(1)} %fusion.1.refs_0_), channel_id=1, source_target_pairs={{0,2},{2,0},{4,6},{6,4},{8,10},{10,8},{12,14},{14,12},{1,3},{3,1},... | collective-permute-start | bytes 786440 | tf_op jit(solution)/shard_map/ppermute | solution.py:339
  192.6 77.0 %collective-permute-start.26 = (bf16[4,32,1024]{2,1,0:T(8,128)(2,1)S(1)}, bf16[4,32,1024]{2,1,0:T(8,128)(2,1)S(1)}, u32[]{:S(2)}, u32[]{:S(2)}) collective-permute-start(bf16[4,32,1024]{2,1,0:T(8,128)(2,1)S(1)} %fusion.refs_0_), channel_id=1, source_target_pairs={{0,1},{1,0},{2,3},{3,2},{4,5},{5,4},{6,7},{7,6},{8,9},{9,8},{10,11... | collective-permute-start | bytes 786440 | tf_op jit(solution)/shard_map/ppermute | solution.py:341
  215.5 21.5 %collective-permute-start.30 = (bf16[3,4,32,1024]{3,2,1,0:T(8,128)(2,1)S(1)}, bf16[3,4,32,1024]{3,2,1,0:T(8,128)(2,1)S(1)}, u32[]{:S(2)}, u32[]{:S(2)}) collective-permute-start(bf16[3,4,32,1024]{3,2,1,0:T(8,128)(2,1)S(1)} %pad_maximum_fusion.refs_1_), channel_id=1, source_target_pairs={{0,2},{2,0},{4,6},{6,4},{8,10},{10,8},{12,14},{14,12},{1,3},{3,1},... | collective-permute-start | bytes 2359304 | tf_op jit(solution)/shard_map/ppermute | solution.py:339
  216.0 21.0 %collective-permute-start.42 = (bf16[3,4,32,1024]{3,2,1,0:T(8,128)(2,1)S(1)}, bf16[3,4,32,1024]{3,2,1,0:T(8,128)(2,1)S(1)}, u32[]{:S(2)}, u32[]{:S(2)}) collective-permute-start(bf16[3,4,32,1024]{3,2,1,0:T(8,128)(2,1)S(1)} %collective-permute-done.40.refs_1_), channel_id=1, source_target_pairs={{0,1},{1,0},{2,3},{3,2},{4,5},{5,4},{6,7},{7,6},{8,9},{9,8},{10,11... | collective-permute-start | bytes 2359304 | tf_op jit(solution)/shard_map/ppermute | solution.py:341
  232.6 37.0 %collective-permute-start.27 = (bf16[3,4,32,1024]{3,2,1,0:T(8,128)(2,1)S(1)}, bf16[3,4,32,1024]{3,2,1,0:T(8,128)(2,1)S(1)}, u32[]{:S(2)}, u32[]{:S(2)}) collective-permute-start(bf16[3,4,32,1024]{3,2,1,0:T(8,128)(2,1)S(1)} %pad_maximum_fusion.1.refs_1_), channel_id=1, source_target_pairs={{0,1},{1,0},{2,3},{3,2},{4,5},{5,4},{6,7},{7,6},{8,9},{9,8},{10,11... | collective-permute-start | bytes 2359304 | tf_op jit(solution)/shard_map/ppermute | solution.py:341
  237.0 83.4 %collective-permute-start.28 = (bf16[4,2,32,2048]{3,2,1,0:T(8,128)(2,1)S(1)}, bf16[4,2,32,2048]{3,2,1,0:T(8,128)(2,1)S(1)}, u32[]{:S(2)}, u32[]{:S(2)}) collective-permute-start(bf16[4,2,32,2048]{3,2,1,0:T(8,128)(2,1)S(1)} %get-tuple-element.33), channel_id=1, source_target_pairs={{0,1},{1,0},{2,3},{3,2},{4,5},{5,4},{6,7},{7,6},{8,9},{9,8},{10,11... | collective-permute-start | bytes 3145736 | tf_op jit(solution)/shard_map/ppermute | solution.py:341
  253.2 32.3 %collective-permute-start.43 = (bf16[4,2,32,2048]{3,2,1,0:T(8,128)(2,1)S(1)}, bf16[4,2,32,2048]{3,2,1,0:T(8,128)(2,1)S(1)}, u32[]{:S(2)}, u32[]{:S(2)}) collective-permute-start(bf16[4,2,32,2048]{3,2,1,0:T(8,128)(2,1)S(1)} %get-tuple-element.43), channel_id=1, source_target_pairs={{0,1},{1,0},{2,3},{3,2},{4,5},{5,4},{6,7},{7,6},{8,9},{9,8},{10,11... | collective-permute-start | bytes 3145736 | tf_op jit(solution)/shard_map/ppermute | solution.py:341
  285.9 26.1 %collective-permute-start.44 = (bf16[4,2,32,2048]{3,2,1,0:T(8,128)(2,1)S(1)}, bf16[4,2,32,2048]{3,2,1,0:T(8,128)(2,1)S(1)}, u32[]{:S(2)}, u32[]{:S(2)}) collective-permute-start(bf16[4,2,32,2048]{3,2,1,0:T(8,128)(2,1)S(1)} %add_convert_fusion), channel_id=1, source_target_pairs={{0,2},{2,0},{4,6},{6,4},{8,10},{10,8},{12,14},{14,12},{1,3},{3,1},... | collective-permute-start | bytes 3145736 | tf_op jit(solution)/shard_map/ppermute | solution.py:339
  286.8 47.1 %collective-permute-start.34 = (bf16[4,2,32,2048]{3,2,1,0:T(8,128)(2,1)S(1)}, bf16[4,2,32,2048]{3,2,1,0:T(8,128)(2,1)S(1)}, u32[]{:S(2)}, u32[]{:S(2)}) collective-permute-start(bf16[4,2,32,2048]{3,2,1,0:T(8,128)(2,1)S(1)} %add_convert_fusion.1), channel_id=1, source_target_pairs={{0,2},{2,0},{4,6},{6,4},{8,10},{10,8},{12,14},{14,12},{1,3},{3,1},... | collective-permute-start | bytes 3145736 | tf_op jit(solution)/shard_map/ppermute | solution.py:339
  313.3 32.6 %collective-permute-start.45 = (bf16[2,32,2048]{2,1,0:T(8,128)(2,1)S(1)}, bf16[2,32,2048]{2,1,0:T(8,128)(2,1)S(1)}, u32[]{:S(2)}, u32[]{:S(2)}) collective-permute-start(bf16[2,32,2048]{2,1,0:T(8,128)(2,1)S(1)} %get-tuple-element.46), channel_id=1, source_target_pairs={{0,4},{2,6},{4,8},{6,10},{8,12},{10,14},{12,0},{14,2},{1,5},{3,7},... | collective-permute-start | bytes 786440 | tf_op jit(solution)/shard_map/ppermute | solution.py:336
  343.9 21.8 %collective-permute-start.47 = (bf16[2,32,2048]{2,1,0:T(8,128)(2,1)S(1)}, bf16[2,32,2048]{2,1,0:T(8,128)(2,1)S(1)}, u32[]{:S(2)}, u32[]{:S(2)}) collective-permute-start(bf16[2,32,2048]{2,1,0:T(8,128)(2,1)S(1)} %get-tuple-element.47), channel_id=1, source_target_pairs={{0,12},{2,14},{4,0},{6,2},{8,4},{10,6},{12,8},{14,10},{1,13},{3,15... | collective-permute-start | bytes 786440 | tf_op jit(solution)/shard_map/ppermute | solution.py:336
  346.0 24.6 %collective-permute-start.46 = (bf16[2,32,2048]{2,1,0:T(8,128)(2,1)S(1)}, bf16[2,32,2048]{2,1,0:T(8,128)(2,1)S(1)}, u32[]{:S(2)}, u32[]{:S(2)}) collective-permute-start(bf16[2,32,2048]{2,1,0:T(8,128)(2,1)S(1)} %add_convert_fusion.3), channel_id=1, source_target_pairs={{0,4},{2,6},{4,8},{6,10},{8,12},{10,14},{12,0},{14,2},{1,5},{3,7},... | collective-permute-start | bytes 786440 | tf_op jit(solution)/shard_map/ppermute | solution.py:336
  (49 other events, 559.9 us)
